TPU v7x, 512 devices: a whole 4x4x16 slice. The times are simulated.
512 devices in a mesh: month: 128 (over z, y, core), col: 4 (over x).
Axes of the slice: x: 4, y: 4, z: 16, core: 2. Of those that a mesh axis runs over, the one named last changes fastest.
Arguments:
- even_inverse: bfloat16 [128, 1024, 1024], P('month', None, 'col'), as said below
- odd_diag: bfloat16 [128, 1024, 1024], P('month', None, 'col'), may hold values from -3 to 3
- lower: bfloat16 [128, 2, 1024, 1024], P('month', None, None, 'col'), may hold values from -0.4375 to 0.4375
- arrow: bfloat16 [128, 64, 1024], P('month', None, 'col'), may hold values from -0.09375 to 0.09375
- odd_arrow: bfloat16 [128, 64, 1024], P('month', None, 'col'), may hold values from -0.09375 to 0.09375
- diag_pattern: int32 [128, 8, 8], P('month'), may hold values 0 or 1
- lower_pattern: int32 [128, 2, 8, 8], P('month'), may hold values 0 or 1
- rhs: bfloat16 [128, 1024, 128], P('month', 'col'), may hold values from -6 to 6
- odd_rhs: bfloat16 [128, 1024, 128], P('month', 'col'), may hold values from -6 to 6
- odd_solution: bfloat16 [128, 1024, 128], P('month', 'col'), may hold values from -6 to 6
- fixed_block: float32 [64, 64], replicated, may hold values from -6 to 6
- fixed_load: float32 [64, 128], replicated, may hold values from -6 to 6
- fixed_solution: bfloat16 [64, 128], replicated, may hold values from -6 to 6
Outputs:
- reduced_diag: float32 [128, 1024, 1024], P('month', None, 'col')
- reduced_lower: float32 [128, 1024, 1024], P('month', None, 'col')
- reduced_arrow: float32 [128, 64, 1024], P('month', None, 'col')
- reduced_rhs: float32 [128, 1024, 128], P('month', 'col')
- reduced_fixed: float32 [64, 64], replicated
- fixed_rhs: float32 [64, 128], replicated
- even_solution: float32 [128, 1024, 128], P('month', 'col')
Inputs may be any that keep to these rules, and one draw needn't show every extreme that they name: even_inverse[j] is symmetric.
All inputs are finite; a program needn't handle non-finite values. No bound on the sum of `diag_pattern` or of `lower_pattern` on one device may be relied on, other than what follows from the above.
Results may differ from a plain program's by a relative error of at most 0.0029.
Values may be sent and summed in bfloat16 or wider, within the bound.
No kernel may reach another device: no remote copies, remote signals or barrier semaphores. Data moves between devices by JAX's collectives and lax.ppermute only.
A program may use at most 128 MiB of HBM per device.

v0:
```python
import functools

import jax
import jax.numpy as jnp
from jax import lax
from jax.sharding import Mesh
from jax.sharding import PartitionSpec as P

TILE = 128
MONTH = ("month_0", "month_1", "month_2")


def passed_along(block, axis, distance):
    devices = range(lax.axis_size(axis))
    route = [(i - distance, i) for i in devices if i - distance in devices]
    return lax.ppermute(block, axis, route)


def in_one_piece(arrays, axis, dim, along):
    both = jnp.concatenate(arrays, axis=along)
    out, at, outs = (lax.all_gather(both, axis, axis=dim, tiled=True), 0, [])
    for a in arrays:
        outs.append(lax.slice_in_dim(out, at, at + a.shape[along], axis=along))
        at += a.shape[along]
    return tuple(outs)


def sent_to_all(array, axis):
    copies = jnp.broadcast_to(array, (lax.axis_size(axis), *array.shape))
    return lax.all_to_all(copies, axis, split_axis=0, concat_axis=0, tiled=True)


def of_everyone(array, axis):
    return sent_to_all(array, axis).sum(axis=0)


def packed_total(arrays, axis):
    ends = [0]
    for a in arrays:
        ends.append(ends[-1] + a.size)
    running = of_everyone(jnp.concatenate([a.ravel() for a in arrays]), axis)
    return tuple((running[b:e].reshape(a.shape) for a, b, e in zip(arrays, ends, ends[1:])))


def one_axis_at_a_time(array, axes):
    return functools.reduce(lax.psum, axes, array)


def tile_mask(pattern):
    return jnp.repeat(jnp.repeat(pattern, TILE, axis=-2), TILE, axis=-1)


def contract(left, right, left_dim, right_dim):
    return lax.dot_general(
        left, right, (((left_dim,), (right_dim,)), ((), ())), preferred_element_type=jnp.float32
    )


def per_device(
    even_inverse,
    odd_diag,
    lower,
    arrow,
    odd_arrow,
    diag_pattern,
    lower_pattern,
    rhs,
    odd_rhs,
    odd_solution,
    fixed_block,
    fixed_load,
    fixed_solution,
):
    col_index = lax.axis_index("col")
    month_index = lax.axis_index(MONTH)
    inverse = even_inverse[0]
    rows_share = odd_diag.shape[2]
    odd_gathered, prev_gathered, weight_full = (
        lax.all_gather(lower[0, 1], "col", axis=1, tiled=True),
        lax.all_gather(lower[0, 0], "col", axis=1, tiled=True),
        lax.all_gather(arrow[0], "col", axis=1, tiled=True),
    )
    exists = (month_index > 0).astype(jnp.bfloat16)
    low_odd = odd_gathered * tile_mask(lower_pattern[0, 1]).astype(jnp.bfloat16)
    low_prev = prev_gathered * tile_mask(lower_pattern[0, 0]).astype(jnp.bfloat16) * exists
    odd_cols = jnp.dot(low_odd, inverse, preferred_element_type=jnp.float32).astype(jnp.bfloat16)
    prev_cols = jnp.dot(low_prev, inverse, preferred_element_type=jnp.float32).astype(jnp.bfloat16)
    arrow_cols = jnp.dot(weight_full, inverse, preferred_element_type=jnp.float32).astype(
        jnp.bfloat16
    )
    odd_rows, prev_rows = (
        lax.all_to_all(odd_cols, "col", split_axis=0, concat_axis=1, tiled=True),
        lax.all_to_all(prev_cols, "col", split_axis=0, concat_axis=1, tiled=True),
    )
    p_term = contract(low_odd, odd_rows, 1, 1)
    q_term = contract(low_prev, prev_rows, 1, 1)
    off_term = -contract(low_odd, prev_rows, 1, 1)
    arrow_here = contract(weight_full, odd_rows, 1, 1)
    arrow_next = contract(weight_full, prev_rows, 1, 1)
    x_odd = odd_solution[0]
    x_prev = passed_along(x_odd, MONTH, 1)
    loads_full, odd_full, prev_full = in_one_piece((rhs[0], x_odd, x_prev), "col", 0, 1)
    rhs_here = jnp.dot(odd_rows, loads_full, preferred_element_type=jnp.float32)
    rhs_next = jnp.dot(prev_rows, loads_full, preferred_element_type=jnp.float32)
    got_diag, got_arrow, got_rhs = passed_along((q_term, arrow_next, rhs_next), MONTH, -1)
    diag_full = tile_mask(diag_pattern[0]).astype(jnp.float32)
    diag_mask = lax.dynamic_slice_in_dim(diag_full, col_index * rows_share, rows_share, 1)
    reduced_diag = odd_diag[0].astype(jnp.float32) * diag_mask - p_term - got_diag
    reduced_arrow = odd_arrow[0].astype(jnp.float32) - arrow_here - got_arrow
    reduced_rhs = odd_rhs[0].astype(jnp.float32) - rhs_here - got_rhs
    y_even = contract(inverse, loads_full, 0, 0)
    weight_local = arrow[0]
    fixed_term = contract(arrow_cols, weight_local, 1, 1)
    load_term = jnp.dot(weight_local.astype(jnp.float32), y_even, precision=lax.Precision.HIGHEST)
    pair_fixed, pair_load = packed_total((fixed_term, load_term), "col")
    fixed_total, load_total = (
        one_axis_at_a_time(pair_fixed, MONTH),
        one_axis_at_a_time(pair_load, MONTH),
    )
    reduced_fixed = fixed_block - fixed_total
    fixed_rhs = fixed_load - load_total
    solved = (
        y_even
        - contract(prev_cols, prev_full, 0, 0)
        - contract(odd_cols, odd_full, 0, 0)
        - contract(arrow_cols, fixed_solution, 0, 0)
    )
    return (
        reduced_diag[None],
        off_term[None],
        reduced_arrow[None],
        reduced_rhs[None],
        reduced_fixed,
        fixed_rhs,
        solved[None],
    )


def solution(mesh):
    finer = Mesh(
        mesh.devices.reshape(16, 4, 2, mesh.shape["col"]), ("month_0", "month_1", "month_2", "col")
    )
    placed = (
        P(MONTH, None, "col"),
        P(MONTH, None, "col"),
        P(MONTH, None, None, "col"),
        P(MONTH, None, "col"),
        P(MONTH, None, "col"),
        P(MONTH, None, None),
        P(MONTH, None, None, None),
        P(MONTH, "col", None),
        P(MONTH, "col", None),
        P(MONTH, "col", None),
        P(),
        P(),
        P(),
    )
    return jax.shard_map(
        per_device,
        mesh=finer,
        in_specs=placed,
        out_specs=(
            P(MONTH, None, "col"),
            P(MONTH, None, "col"),
            P(MONTH, None, "col"),
            P(MONTH, "col", None),
            P(),
            P(),
            P(MONTH, "col", None),
        ),
        check_vma=False,
    )
```

profile of v0, /device:TPU:1, one launch (start us, length us, event | category | flops | bytes accessed | tf_op | source)
XLA Modules:
  0.0 203.6 jit_solution(1457841014159792766)
XLA Ops:
  7.3 2.3 %fusion.31 = (bf16[1,1,1024,256]{3,2,1,0:T(8,128)(2,1)}, bf16[1,1,1024,256]{3,2,1,0:T(8,128)(2,1)}) fusion(bf16[1,2,1024,256]{3,2,1,0:T(8,128)(2,1)} %param.15), kind=kLoop, calls=%fused_computation.50 | loop fusion | bytes 2097152 | tf_op jit(solution)/shard_map/slice | solution.py:79
  10.4 4.6 %collective-permute-start.2 = (bf16[256,128]{1,0:T(8,128)(2,1)S(1)}, bf16[256,128]{1,0:T(8,128)(2,1)S(1)}, u32[]{:S(2)}, u32[]{:S(2)}) collective-permute-start(bf16[256,128]{1,0:T(8,128)(2,1)S(1)} %bitcast.131), channel_id=1, source_target_pairs={{0,4},{4,8},{8,12},{12,16},{16,20},{20,24},{24,28},{28,32},{32,36}... | collective-permute-start | bytes 196616 | tf_op jit(solution)/shard_map/ppermute | solution.py:16
  15.0 9.6 %all-gather.2 = bf16[1,64,1024]{2,1,0:T(8,128)(2,1)S(1)} all-gather(bf16[1,64,256]{2,1,0:T(8,128)(2,1)S(1)} %copy-done.12), channel_id=4, replica_groups=mesh['month_0'=16,'month_1'=4,'month_2'=2,'col'=4] {'col'}, dimensions={2}, use_global_device_ids=true | all-gather | bytes 163840 | tf_op jit(solution)/shard_map/all_gather | solution.py:81
  24.9 0.9 fusion.32
  25.9 1.1 broadcast_in_dim.37
  27.1 3.0 %copy.60 = f32[128,8,8,128]{3,1,2,0:T(8,128)} copy(f32[128,8,8,128]{3,2,1,0:T(8,128)S(1)} %bitcast.116) | data formatting | bytes 8388608
  30.1 15.1 %all_gather.15 = bf16[1024,384]{1,0:T(8,128)(2,1)S(1)} all-gather(bf16[256,384]{1,0:T(8,128)(2,1)S(1)} %pad_maximum_fusion), channel_id=1, replica_groups=mesh['month_0'=16,'month_1'=4,'month_2'=2,'col'=4] {'col'}, dimensions={0}, use_global_device_ids=true | all-gather | bytes 983040 | tf_op jit(solution)/shard_map/all_gather | solution.py:21
  45.7 0.8 broadcast_in_dim.46
  46.5 3.4 %all-to-all-start.2 = ((f32[4,1,12288]{2,1,0:T(1,128)}), f32[4,1,12288]{2,1,0:T(1,128)S(1)}, u32[]{:S(2)}, u32[]{:S(2)}) async-start(f32[4,1,12288]{2,1,0:T(1,128)} %broadcast_in_dim.46), calls=%async_computation.2 | async-start | bytes 393216 | tf_op jit(solution)/shard_map/all_to_all | solution.py:30
  49.8 7.0 %all-to-all-done.2 = f32[4,1,12288]{2,1,0:T(1,128)S(1)} async-done(((f32[4,1,12288]{2,1,0:T(1,128)}), f32[4,1,12288]{2,1,0:T(1,128)S(1)}, u32[]{:S(2)}, u32[]{:S(2)}) %all-to-all-start.2) | async-done | bytes 196640 | tf_op jit(solution)/shard_map/all_to_all | solution.py:30
  57.1 50.2 %all-reduce = (f32[64,64]{1,0:T(8,128)S(1)}, f32[64,128]{1,0:T(8,128)S(1)}) all-reduce(f32[64,64]{1,0:T(8,128)S(1)} %reshape.73, f32[64,128]{1,0:T(8,128)S(1)} %slice_bitcast_fusion), channel_id=1, replica_groups=mesh['month_0'=16,'month_1'=4,'month_2'=2,'col'=4] {'month_0'}, use_global_device_ids=true, to_apply=%region_1.0 | all-reduce | flops 12288 | bytes 98304 | tf_op jit(solution)/shard_map/psum | solution.py:46
  107.4 12.9 %all-reduce.1 = (f32[64,64]{1,0:T(8,128)S(1)}, f32[64,128]{1,0:T(8,128)S(1)}) all-reduce(f32[64,64]{1,0:T(8,128)S(1)} %get-tuple-element.35, f32[64,128]{1,0:T(8,128)S(1)} %get-tuple-element.36), channel_id=1, replica_groups=mesh['month_0'=16,'month_1'=4,'month_2'=2,'col'=4] {'month_1'}, use_global_device_ids=true, to_apply=%region_2.0 | all-reduce | flops 12288 | bytes 98304 | tf_op jit(solution)/shard_map/psum | solution.py:46
  120.3 23.1 %all-reduce.2 = (f32[64,64]{1,0:T(8,128)S(1)}, f32[64,128]{1,0:T(8,128)S(1)}) all-reduce(f32[64,64]{1,0:T(8,128)S(1)} %get-tuple-element.37, f32[64,128]{1,0:T(8,128)S(1)} %get-tuple-element.38), channel_id=1, replica_groups=mesh['month_0'=16,'month_1'=4,'month_2'=2,'col'=4] {'month_2'}, use_global_device_ids=true, to_apply=%region_3.0 | all-reduce | flops 12288 | bytes 98304 | tf_op jit(solution)/shard_map/psum | solution.py:46
  144.7 2.9 %broadcast_in_dim.41 = bf16[1024,8,128]{2,1,0:T(8,128)(2,1)S(1)} broadcast(bf16[1024,8]{1,0:T(8,128)(2,1)S(1)} %bitcast.129), dimensions={0,1} | broadcast | bytes 2113536 | tf_op jit(solution)/shard_map/broadcast_in_dim | solution.py:50
  149.1 1.0 copy.37
  150.1 4.1 %all-to-all-start.1 = ((bf16[4,256,256]{1,2,0:T(8,128)(2,1)}), bf16[4,256,256]{1,2,0:T(8,128)(2,1)}, u32[]{:S(2)}, u32[]{:S(2)}) async-start(bf16[4,256,256]{1,2,0:T(8,128)(2,1)} %copy.37), calls=%async_computation.1 | async-start | bytes 1048576 | tf_op jit(solution)/shard_map/all_to_all | solution.py:93
  154.3 2.9 %broadcast_in_dim.39 = bf16[1024,8,128]{2,1,0:T(8,128)(2,1)S(1)} broadcast(bf16[1024,8]{1,0:T(8,128)(2,1)S(1)} %bitcast.130), dimensions={0,1} | broadcast | bytes 2113536 | tf_op jit(solution)/shard_map/broadcast_in_dim | solution.py:50
  159.1 0.9 fusion.5
  160.1 1.7 copy.42
  161.7 2.0 %copy.36 = bf16[4,256,256]{1,2,0:T(8,128)(2,1)} copy(bf16[4,256,256]{2,1,0:T(8,128)(2,1)} %bitcast.128) | data formatting | bytes 1048576 | tf_op jit(solution)/shard_map/all_to_all | solution.py:92
  163.8 4.2 %all-to-all-start = ((bf16[4,256,256]{1,2,0:T(8,128)(2,1)}), bf16[4,256,256]{1,2,0:T(8,128)(2,1)S(1)}, u32[]{:S(2)}, u32[]{:S(2)}) async-start(bf16[4,256,256]{1,2,0:T(8,128)(2,1)} %copy.36), calls=%async_computation | async-start | bytes 1048576 | tf_op jit(solution)/shard_map/all_to_all | solution.py:92
  167.9 4.1 %fusion.16 = f32[1024,256]{1,0:T(8,128)} fusion(bf16[256,1024]{0,1:T(8,128)(2,1)} %bitcast.15, bf16[128,8,8,128]{3,2,1,0:T(8,128)(2,1)} %bitcast.126, bf16[1,1,1024,1024]{3,2,1,0:T(8,128)(2,1)} %all-gather.8.cloned.1.call-done, bf16[]{:T(256)S(6)} %convert_element_type.82), kind=kOutput, calls=%fused_computation.31 | convolution fusion | flops 538968064 | bytes 5767170 | tf_op jit(solution)/shard_map/dot_general | solution.py:54
  172.1 2.6 %collective-permute-start = (f32[1024,256]{1,0:T(8,128)}, f32[1024,256]{1,0:T(8,128)}, u32[]{:S(2)}, u32[]{:S(2)}) collective-permute-start(f32[1024,256]{1,0:T(8,128)} %fusion.16), channel_id=1, source_target_pairs={{4,0},{8,4},{12,8},{16,12},{20,16},{24,20},{28,24},{32,28},{36,32}... | collective-permute-start | bytes 3145736 | tf_op jit(solution)/shard_map/ppermute | solution.py:16
  174.7 1.9 convolution_bitcast_fusion
  176.6 1.9 collective-permute-start.1
  178.5 1.4 fusion.22
  180.0 1.9 collective-permute-start.3
  181.9 2.7 %fusion.1 = f32[1,1024,256]{2,1,0:T(8,128)} fusion(bf16[256,1024]{0,1:T(8,128)(2,1)} %bitcast.15, bf16[128,8,8,128]{3,2,1,0:T(8,128)(2,1)S(1)} %bitcast.121, bf16[1,1,1024,1024]{3,2,1,0:T(8,128)(2,1)S(1)} %copy-done.7), kind=kOutput, calls=%fused_computation.5 | convolution fusion | flops 538181632 | bytes 5767168 | tf_op jit(solution)/shard_map/dot_general | solution.py:54
  184.7 4.6 %collective-permute-done.1 = f32[64,256]{1,0:T(8,128)} collective-permute-done((f32[64,256]{1,0:T(8,128)}, f32[64,256]{1,0:T(8,128)}, u32[]{:S(2)}, u32[]{:S(2)}) %collective-permute-start.1) | collective-permute-done | bytes 65568 | tf_op jit(solution)/shard_map/ppermute | solution.py:16
  189.2 1.7 fusion.10
  190.9 2.0 fusion.7
  192.8 3.9 %fusion.3 = f32[1,1024,256]{2,1,0:T(8,128)} fusion(f32[1024,256]{1,0:T(8,128)} %collective-permute-done, bf16[256,1024]{0,1:T(8,128)(2,1)S(1)} %bitcast.119, f32[1024,1024]{1,0:T(8,128)} %bitcast.123, s32[]{:T(128)S(6)} %select_n.3, bf16[1,1024,256]{2,1,0:T(8,128)(2,1)S(1)} %copy-done.10, bf16[128,8,8,128]{3,2,1,0:T(8,128)(2,1)S(1)} %bitcast.122, ...), kind=kOutput, calls=%fused_computation.8 | convolution fusion | flops 538968064 | bytes 8388612 | tf_op jit(solution)/shard_map/dot_general | solution.py:54
  (75 shorter events, 6.6 us)
Async XLA Ops:
  7.2 17.4 %copy-start = (bf16[1,1024,256]{2,1,0:T(8,128)(2,1)S(1)}, bf16[1,1024,256]{2,1,0:T(8,128)(2,1)}, u32[]{:S(2)}) copy-start(bf16[1,1024,256]{2,1,0:T(8,128)(2,1)} %param.13) | copy-start | bytes 1572868
  7.2 3.2 %copy-start.13 = (bf16[1,256,128]{2,1,0:T(8,128)(2,1)S(1)}, bf16[1,256,128]{2,1,0:T(8,128)(2,1)}, u32[]{:S(2)}) copy-start(bf16[1,256,128]{2,1,0:T(8,128)(2,1)} %param.22) | copy-start | bytes 196612
  7.2 7.8 %copy-start.12 = (bf16[1,64,256]{2,1,0:T(8,128)(2,1)S(1)}, bf16[1,64,256]{2,1,0:T(8,128)(2,1)}, u32[]{:S(2)}) copy-start(bf16[1,64,256]{2,1,0:T(8,128)(2,1)} %param.16) | copy-start | bytes 98308
  7.2 17.7 %copy-start.17 = (bf16[64,128]{1,0:T(8,128)(2,1)S(1)}, bf16[64,128]{1,0:T(8,128)(2,1)}, u32[]{:S(2)}) copy-start(bf16[64,128]{1,0:T(8,128)(2,1)} %param.25) | copy-start | bytes 49156
  7.2 18.6 %copy-start.19 = (s32[1,8,8]{2,1,0:T(8,128)S(1)}, s32[1,8,8]{2,1,0:T(8,128)}, u32[]{:S(2)}) copy-start(s32[1,8,8]{2,1,0:T(8,128)} %param.18) | copy-start | bytes 772
  7.2 18.6 %copy-start.18 = (s32[1,2,8,8]{3,2,1,0:T(8,128)S(1)}, s32[1,2,8,8]{3,2,1,0:T(8,128)}, u32[]{:S(2)}) copy-start(s32[1,2,8,8]{3,2,1,0:T(8,128)} %param.19) | copy-start | bytes 1540
  7.2 137.5 %all-gather.8.cloned.1.call-start = ((), (), s32[]{:S(2)}) async-start(), calls=%async_computation.4 | async-start | bytes 2621440 | tf_op jit(solution)/shard_map/all_gather | solution.py:80
  9.6 144.6 %all-gather.6.cloned.1.call-start = ((), (), s32[]{:S(2)}) async-start(), calls=%async_computation.3 | async-start | bytes 2621440 | tf_op jit(solution)/shard_map/all_gather | solution.py:79
  10.4 19.7 %collective-permute-start.2 = (bf16[256,128]{1,0:T(8,128)(2,1)S(1)}, bf16[256,128]{1,0:T(8,128)(2,1)S(1)}, u32[]{:S(2)}, u32[]{:S(2)}) collective-permute-start(bf16[256,128]{1,0:T(8,128)(2,1)S(1)} %bitcast.131), channel_id=1, source_target_pairs={{0,4},{4,8},{8,12},{12,16},{16,20},{20,24},{24,28},{28,32},{32,36}... | collective-permute-start | bytes 196616 | tf_op jit(solution)/shard_map/ppermute | solution.py:16
  27.1 3.0 %copy-start.14 = (bf16[1,256,128]{2,1,0:T(8,128)(2,1)S(1)}, bf16[1,256,128]{2,1,0:T(8,128)(2,1)}, u32[]{:S(2)}) copy-start(bf16[1,256,128]{2,1,0:T(8,128)(2,1)} %param.20) | copy-start | bytes 196612
  30.1 113.4 %copy-start.15 = (f32[64,64]{1,0:T(8,128)S(1)}, f32[64,64]{1,0:T(8,128)}, u32[]{:S(2)}) copy-start(f32[64,64]{1,0:T(8,128)} %param.23) | copy-start | bytes 49156
  30.1 114.0 %copy-start.16 = (f32[64,128]{1,0:T(8,128)S(1)}, f32[64,128]{1,0:T(8,128)}, u32[]{:S(2)}) copy-start(f32[64,128]{1,0:T(8,128)} %param.24) | copy-start | bytes 98308
  45.2 113.5 %copy-start.1 = (bf16[1024,384]{1,0:T(8,128)(2,1)}, bf16[1024,384]{1,0:T(8,128)(2,1)S(1)}, u32[]{:S(2)}) copy-start(bf16[1024,384]{1,0:T(8,128)(2,1)S(1)} %all_gather.15) | copy-start | bytes 2359300
  45.4 102.3 %copy-start.8 = (f32[128,256]{1,0:T(8,128)}, f32[128,256]{1,0:T(8,128)S(1)}, u32[]{:S(2)}) copy-start(f32[128,256]{1,0:T(8,128)S(1)} %fusion.11) | copy-start | bytes 393220
  46.5 10.4 %all-to-all-start.2 = ((f32[4,1,12288]{2,1,0:T(1,128)}), f32[4,1,12288]{2,1,0:T(1,128)S(1)}, u32[]{:S(2)}, u32[]{:S(2)}) async-start(f32[4,1,12288]{2,1,0:T(1,128)} %broadcast_in_dim.46), calls=%async_computation.2 | async-start | bytes 393216 | tf_op jit(solution)/shard_map/all_to_all | solution.py:30
  144.7 3.0 %copy-start.20 = (bf16[1,1,1024,1024]{3,2,1,0:T(8,128)(2,1)S(1)}, bf16[1,1,1024,1024]{3,2,1,0:T(8,128)(2,1)}, u32[]{:S(2)}) copy-start(bf16[1,1,1024,1024]{3,2,1,0:T(8,128)(2,1)} %all-gather.8.cloned.1.call-done) | copy-start | bytes 6291460
  147.7 1.4 copy-start.2
  149.1 5.2 %copy-start.3 = (bf16[1024,256]{1,0:T(8,128)(2,1)}, bf16[1024,256]{1,0:T(8,128)(2,1)S(1)}, u32[]{:S(2)}) copy-start(bf16[1024,256]{1,0:T(8,128)(2,1)S(1)} %convolution_convert_fusion) | copy-start | bytes 1572868
  150.1 13.7 %all-to-all-start.1 = ((bf16[4,256,256]{1,2,0:T(8,128)(2,1)}), bf16[4,256,256]{1,2,0:T(8,128)(2,1)}, u32[]{:S(2)}, u32[]{:S(2)}) async-start(bf16[4,256,256]{1,2,0:T(8,128)(2,1)} %copy.37), calls=%async_computation.1 | async-start | bytes 1048576 | tf_op jit(solution)/shard_map/all_to_all | solution.py:93
  154.3 3.0 %copy-start.6 = (bf16[1,1,1024,1024]{3,2,1,0:T(8,128)(2,1)S(1)}, bf16[1,1,1024,1024]{3,2,1,0:T(8,128)(2,1)}, u32[]{:S(2)}) copy-start(bf16[1,1,1024,1024]{3,2,1,0:T(8,128)(2,1)} %all-gather.6.cloned.1.call-done) | copy-start | bytes 6291460
  157.3 1.0 copy-start.4
  157.3 1.1 copy-start.9
  157.3 1.8 copy-start.11
  158.3 0.8 copy-start.5
  163.8 20.9 %all-to-all-start = ((bf16[4,256,256]{1,2,0:T(8,128)(2,1)}), bf16[4,256,256]{1,2,0:T(8,128)(2,1)S(1)}, u32[]{:S(2)}, u32[]{:S(2)}) async-start(bf16[4,256,256]{1,2,0:T(8,128)(2,1)} %copy.36), calls=%async_computation | async-start | bytes 1048576 | tf_op jit(solution)/shard_map/all_to_all | solution.py:92
  167.9 14.0 %copy-start.7 = (bf16[1,1,1024,1024]{3,2,1,0:T(8,128)(2,1)S(1)}, bf16[1,1,1024,1024]{3,2,1,0:T(8,128)(2,1)}, u32[]{:S(2)}) copy-start(bf16[1,1,1024,1024]{3,2,1,0:T(8,128)(2,1)} %all-gather.6.cloned.1.call-done) | copy-start | bytes 6291460
  172.1 20.8 %collective-permute-start = (f32[1024,256]{1,0:T(8,128)}, f32[1024,256]{1,0:T(8,128)}, u32[]{:S(2)}, u32[]{:S(2)}) collective-permute-start(f32[1024,256]{1,0:T(8,128)} %fusion.16), channel_id=1, source_target_pairs={{4,0},{8,4},{12,8},{16,12},{20,16},{24,20},{28,24},{32,28},{36,32}... | collective-permute-start | bytes 3145736 | tf_op jit(solution)/shard_map/ppermute | solution.py:16
  176.6 12.6 %collective-permute-start.1 = (f32[64,256]{1,0:T(8,128)}, f32[64,256]{1,0:T(8,128)}, u32[]{:S(2)}, u32[]{:S(2)}) collective-permute-start(f32[64,256]{1,0:T(8,128)} %convolution_bitcast_fusion), channel_id=1, source_target_pairs={{4,0},{8,4},{12,8},{16,12},{20,16},{24,20},{28,24},{32,28},{36,32}... | collective-permute-start | bytes 196616 | tf_op jit(solution)/shard_map/ppermute | solution.py:16
  180.0 10.9 %collective-permute-start.3 = (f32[256,128]{1,0:T(8,128)S(1)}, f32[256,128]{1,0:T(8,128)S(1)}, u32[]{:S(2)}, u32[]{:S(2)}) collective-permute-start(f32[256,128]{1,0:T(8,128)S(1)} %fusion.22), channel_id=1, source_target_pairs={{4,0},{8,4},{12,8},{16,12},{20,16},{24,20},{28,24},{32,28},{36,32}... | collective-permute-start | bytes 393224 | tf_op jit(solution)/shard_map/ppermute | solution.py:16
  184.6 8.2 %copy-start.10 = (bf16[1,1024,256]{2,1,0:T(8,128)(2,1)S(1)}, bf16[1,1024,256]{2,1,0:T(8,128)(2,1)}, u32[]{:S(2)}) copy-start(bf16[1,1024,256]{2,1,0:T(8,128)(2,1)} %param.14) | copy-start | bytes 1572868
Sparse Core Ops, SparseCore 0:
  10.7 52.0 all-gather.7
  65.5 42.2 all-gather.5
where the time goes:
time: 204 us
  blocking collectives  111 us (54%)
  starting transfers between devices  22.8 us (11%)
  matrix products  22.1 us (11%)
  local copies, waits for them, and re-layouts  19.5 us (10%)
  between operations  14.4 us (7%)
  waiting for transfers between devices  12.3 us (6%)
    psum x3, blocking collectives, one_axis_at_a_time(): return functools.reduce(lax.psum, axes, array)  86.3 us
    dot_general x10, matrix products, contract(): lax.dot_general(left, right, (((left_dim,), (right_dim,)), ((), ())), pre...  16.8 us
    all_gather x1, blocking collectives, in_one_piece(): out, at, outs = (lax.all_gather(both, axis, axis=dim, tiled=True), 0, [])  15.1 us
    ppermute x4, starting transfers between devices, passed_along(): return lax.ppermute(block, axis, route)  11 us
    all_gather x1, blocking collectives, per_device(): lax.all_gather(arrow[0], 'col', axis=1, tiled=True)  9.61 us
    broadcast_in_dim x6, local copies, waits for them, and re-layouts, tile_mask(): return jnp.repeat(jnp.repeat(pattern, TILE, axis=-2), TILE, axis=-1)  7.13 us
    all_to_all x1, waiting for transfers between devices, sent_to_all(): return lax.all_to_all(copies, axis, split_axis=0, concat_axis=0, tiled=True)  7.04 us
    unnamed x44, local copies, waits for them, and re-layouts  6.12 us
  transfers between devices with their start and end apart: 9, of which 2 were waited for; matrix products, arithmetic and copies ran while one was open for 17% of the time, Pallas kernels for 0%

commit v1 on v0

v1 whole, which is shorter than its diff:
```python
import jax
import jax.numpy as jnp
from jax import lax
from jax.experimental import pallas as pl
from jax.experimental.pallas import tpu as pltpu
from jax.sharding import Mesh
from jax.sharding import PartitionSpec as P


MONTH = ("month_z", "month_y", "month_k")
BF = jnp.bfloat16
F32 = jnp.float32
T = 128
S = 256
R = 1024
SLOTS = 16
SHARE = SLOTS + 6
CUT = 9
TO_RIGHT = SHARE + 8
TO_LEFT = SHARE + 12
STACK = R + T + 64


def shifted(block, distance):
    n = lax.axis_size(MONTH)
    route = [(i, i + distance) for i in range(n) if 0 <= i + distance < n]
    return lax.ppermute(block, MONTH, route)


def exchanged(pieces, axis):
    return lax.all_to_all(pieces, axis, split_axis=0, concat_axis=0, tiled=True)


def sent_to_all(array, axis):
    return exchanged(jnp.broadcast_to(array, (lax.axis_size(axis), *array.shape)), axis)


def nn(a, b):
    return lax.dot_general(a, b, (((1,), (0,)), ((), ())), preferred_element_type=F32)


def nt(a, b):
    return lax.dot_general(a, b, (((1,), (1,)), ((), ())), preferred_element_type=F32)


def full(shape):
    return pl.BlockSpec(shape, lambda *_: (0,) * len(shape))


def flipped(x):
    return x.astype(F32).T


def call(body, grid, scalars, in_specs, out_specs, out_shape, scratch=()):
    return pl.pallas_call(
        body,
        grid_spec=pltpu.PrefetchScalarGridSpec(
            num_scalar_prefetch=scalars,
            grid=grid,
            in_specs=in_specs,
            out_specs=out_specs,
            scratch_shapes=list(scratch),
        ),
        out_shape=out_shape,
    )


def at_tile(n, count=1):
    return slice(n * T, (n + count) * T)


def pack_body(pos_ref, pat_ref, low_ref, e_ref, b_ref, x_ref, xp_ref, right_ref, left_ref):
    c = pos_ref[0]
    slot = jnp.int32(0)
    for kind in range(2):
        for r in range(8):
            for k in range(2):
                there = pat_ref[kind, r, 2 * c + k] > 0

                @pl.when(there & (slot < SLOTS))
                def _(slot=slot, kind=kind, r=r, k=k):
                    tile = low_ref[0, kind, r * T : (r + 1) * T, k * T : (k + 1) * T]
                    right_ref[pl.ds(pl.multiple_of(slot * T, T), T), :] = tile
                    left_ref[pl.ds(pl.multiple_of((slot + 4) * T, T), T), :] = tile

                slot = slot + there.astype(jnp.int32)
    for n, ref in enumerate((b_ref, x_ref, xp_ref)):
        for k in range(2):
            tile = flipped(ref[0, k * T : (k + 1) * T]).astype(BF)
            right_ref[at_tile(SLOTS + 2 * n + k)] = tile
            left_ref[at_tile(4 + SLOTS + 2 * n + k)] = tile
    for ref, places in (
        (right_ref, ((0, SHARE), (3, SHARE + 4))),
        (left_ref, ((0, 0), (1, SHARE + 4), (2, SHARE + 8))),
    ):
        for off, place in places:
            rows = pl.ds(pl.multiple_of(lax.rem(c + off, 4) * S, S), S)
            for k in range(2):
                ref[at_tile(place + 2 * k, 2)] = e_ref[0, rows, k * T : (k + 1) * T]


def packed(pos, pattern, lower, inverse, rhs, x_odd, x_prev):
    return call(
        pack_body, (1,), 2,
        [full((1, 2, R, S)), full((1, R, S))] + [full((1, S, T))] * 3,
        [full((TO_RIGHT * T, T)), full((TO_LEFT * T, T))],
        (
            jax.ShapeDtypeStruct((TO_RIGHT * T, T), BF),
            jax.ShapeDtypeStruct((TO_LEFT * T, T), BF),
        ),
    )(pos, pattern, lower, inverse, rhs, x_odd, x_prev)


class Shares:
    def __init__(self, pos_ref, own, left, right, far_k0, far_k1, e_ref, wg_ref, far_tiles):
        self.c = pos_ref[0]
        self.refs = {0: (own, 0), 1: (right, 4), 2: (far_tiles, 0), 3: (left, 0)}
        self.left, self.right, self.far_k0, self.far_k1 = left, right, far_k0, far_k1
        self.e_ref, self.wg_ref = e_ref, wg_ref
        far_tiles[at_tile(0, CUT)] = far_k1[at_tile(2, CUT)]
        far_tiles[at_tile(CUT, SHARE - CUT)] = far_k0[at_tile(0, SHARE - CUT)]

    def source(self, r):
        return lax.rem(self.c + r, 4)

    def rows(self, r):
        return pl.ds(pl.multiple_of(self.source(r) * S, S), S)

    def tile(self, r, n):
        ref, first = self.refs[r]
        return ref[pl.ds(pl.multiple_of((n + first) * T, T), T), :]

    def vector(self, r, which):
        ref, first = self.refs[r]
        n = first + SLOTS + 2 * which
        return jnp.concatenate([ref[at_tile(n)], ref[at_tile(n + 1)]], axis=1)

    def weight(self, r):
        return self.wg_ref[self.source(r)]

    def unpack(self, pat_ref, kind, live, stack):
        for r in range(4):
            source = self.source(r)
            slot = jnp.int32(0)
            if kind:
                for i in range(8):
                    for k in range(2):
                        slot = slot + pat_ref[0, i, 2 * source + k]
            for i in range(8):
                for k in range(2):
                    there = pat_ref[kind, i, 2 * source + k] > 0
                    tile = self.tile(r, jnp.minimum(slot, SLOTS - 1))
                    keep = there if live is None else there & (live > 0)
                    cols = slice(r * S + k * T, r * S + (k + 1) * T)
                    stack[i * T : (i + 1) * T, cols] = jnp.where(
                        keep, tile, jnp.zeros_like(tile)
                    )
                    slot = slot + there.astype(jnp.int32)
            stack[R : R + T, r * S : (r + 1) * S] = self.vector(r, 0)
            stack[R + T :, r * S : (r + 1) * S] = self.weight(r)

    def stored(self, r1, r2):
        if r2 == 0:
            return self.e_ref[0, self.rows(r1), :]
        if (r1, r2) == (2, 2):
            halves = [
                self.far_k0[at_tile(SHARE - CUT, 2)],
                self.far_k1[at_tile(0, 2)],
            ]
        else:
            ref, n = {
                (1, 1): (self.right, 0),
                (2, 1): (self.right, 4 + SHARE),
                (3, 1): (self.right, 8 + SHARE),
                (3, 3): (self.left, SHARE),
                (2, 3): (self.left, SHARE + 4),
            }[r1, r2]
            halves = [ref[at_tile(n, 2)], ref[at_tile(n + 2, 2)]]
        return jnp.concatenate(halves, axis=1)

    def times_inverse(self, block, r2):
        total = None
        for r1 in range(4):
            part = block[:, r1 * S : (r1 + 1) * S]
            if r2 == 0 or (r1, r2) in ((1, 1), (2, 1), (3, 1), (2, 2), (2, 3), (3, 3)):
                part = nn(part, self.stored(r1, r2))
            else:
                part = nt(part, self.stored(r2, r1))
            total = part if total is None else total + part
        return total

    def applied(self, which, stack):
        total = None
        for r in range(4):
            part = nn(self.vector(r, which), stack[self.rows(r), :])
            total = part if total is None else total + part
        return total


SHARE_SPECS = [
    full((TO_RIGHT * T, T)), full((TO_RIGHT * T, T)), full((TO_LEFT * T, T)),
    full(((SHARE - CUT + 2) * T, T)), full(((CUT + 2) * T, T)),
    full((1, R, S)), full((4, 64, S)),
]
SHARE_SCRATCH = [pltpu.VMEM((SHARE * T, T), BF), pltpu.VMEM((STACK, R), BF)]


def next_body(pos_ref, pat_ref, *refs):
    ahead_ref, v_ref, z_ref, far_tiles, stack = refs[7:]
    shares = Shares(pos_ref, *refs[:7], far_tiles)
    shares.unpack(pat_ref, 0, pos_ref[1], stack)
    low = stack[shares.rows(0), :]
    for r in range(4):
        v_ref[:, r * S : (r + 1) * S] = shares.times_inverse(low, r).astype(BF)
    ahead_ref[...] = nt(stack[...], v_ref[...]).astype(BF)
    z_ref[...] = shares.applied(2, stack)


def next_terms(pos, pattern, shares, inverse, wg):
    return call(
        next_body, (1,), 2, SHARE_SPECS,
        [full((STACK, S)), full((S, R)), full((T, R))],
        (
            jax.ShapeDtypeStruct((STACK, S), BF),
            jax.ShapeDtypeStruct((S, R), BF),
            jax.ShapeDtypeStruct((T, R), F32),
        ),
        SHARE_SCRATCH,
    )(pos, pattern, *shares, inverse, wg)


def here_body(pos_ref, pat_ref, *refs):
    v_ref, z_ref, f_ref, here_ref, off_ref, solved_ref, far_tiles, stack, u_rows = refs[7:]
    shares = Shares(pos_ref, *refs[:7], far_tiles)
    shares.unpack(pat_ref, 1, None, stack)
    low = stack[shares.rows(0), :]
    for r in range(4):
        u_rows[:, r * S : (r + 1) * S] = shares.times_inverse(low, r).astype(BF)
    here_ref[...] = nt(stack[...], u_rows[...])
    off_ref[0] = -nt(stack[:R], v_ref[...])
    z = z_ref[...] + shares.applied(1, stack)
    fixed = flipped(f_ref[...]).astype(BF)
    z = z + nn(fixed, stack[R + T :])
    rest = stack[R : R + T].astype(F32) - z
    high = rest.astype(BF)
    low_part = (rest - high.astype(F32)).astype(BF)
    total = None
    for r in range(4):
        cols = slice(r * S, (r + 1) * S)
        block = shares.stored(r, 0)
        part = nn(high[:, cols], block) + nn(low_part[:, cols], block)
        total = part if total is None else total + part
    solved_ref[0] = total.T


def here_terms(pos, pattern, shares, inverse, wg, v_rows, z, fixed):
    return call(
        here_body, (1,), 2,
        SHARE_SPECS + [full((S, R)), full((T, R)), full((64, T))],
        [full((STACK, S)), full((1, R, S)), full((1, S, T))],
        (
            jax.ShapeDtypeStruct((STACK, S), F32),
            jax.ShapeDtypeStruct((1, R, S), F32),
            jax.ShapeDtypeStruct((1, S, T), F32),
        ),
        SHARE_SCRATCH + [pltpu.VMEM((S, R), BF)],
    )(pos, pattern, *shares, inverse, wg, v_rows, z, fixed)


def reduced_body(
    pos_ref, dpat_ref, here_ref, got_ref, diag_ref, oarrow_ref, orhs_ref, rd_ref, ra_ref, rr_ref
):
    c = pos_ref[0]
    for i in range(8):
        for k in range(2):
            keep = dpat_ref[i, 2 * c + k] > 0
            rs, cs = slice(i * T, (i + 1) * T), slice(k * T, (k + 1) * T)
            tile = diag_ref[0, rs, cs].astype(F32)
            total = here_ref[rs, cs] + got_ref[rs, cs].astype(F32)
            rd_ref[0, rs, cs] = jnp.where(keep, tile, jnp.zeros_like(tile)) - total
    tail = here_ref[R:] + got_ref[R:].astype(F32)
    rr_ref[0] = orhs_ref[0].astype(F32) - tail[:T].T
    ra_ref[0] = oarrow_ref[0].astype(F32) - tail[T:]


def reduced_terms(pos, dpattern, here, got, diag, oarrow, orhs):
    return call(
        reduced_body, (1,), 2,
        [
            full((STACK, S)), full((STACK, S)), full((1, R, S)),
            full((1, 64, S)), full((1, S, T)),
        ],
        [full((1, R, S)), full((1, 64, S)), full((1, S, T))],
        (
            jax.ShapeDtypeStruct((1, R, S), F32),
            jax.ShapeDtypeStruct((1, 64, S), F32),
            jax.ShapeDtypeStruct((1, S, T), F32),
        ),
    )(pos, dpattern, here, got, diag, oarrow, orhs)


def spread_body(pieces_ref, out_ref):
    total = pieces_ref[0]
    for n in range(1, pieces_ref.shape[0]):
        total = total + pieces_ref[n]
    for n in range(out_ref.shape[0]):
        out_ref[n] = total


def spread(pieces, copies):
    shape = pieces.shape[1:]
    return call(
        spread_body, (1,), 0, [full(pieces.shape)], full((copies, *shape)),
        jax.ShapeDtypeStruct((copies, *shape), F32),
    )(pieces)


def settle_body(pieces_ref, block_ref, load_ref, fixed_ref, rhs_ref, over_ref):
    for n in range(8):
        total = pieces_ref[4 * n]
        for k in range(1, 4):
            total = total + pieces_ref[4 * n + k]
        if n < 4:
            rows = slice(16 * n, 16 * n + 16)
            fixed_ref[rows] = block_ref[rows] - total[:, :64]
        else:
            rows = slice(16 * n - 64, 16 * n - 48)
            rhs_ref[rows] = load_ref[rows] - total
        if n == 0:
            over_ref[...] = total[:8]


def settled(pieces, fixed_block, fixed_load):
    return call(
        settle_body, (1,), 0,
        [full((32, 16, 128)), full((64, 64)), full((64, 128))],
        [full((64, 64)), full((64, 128)), full((8, 128))],
        (
            jax.ShapeDtypeStruct((64, 64), F32),
            jax.ShapeDtypeStruct((64, 128), F32),
            jax.ShapeDtypeStruct((8, 128), F32),
        ),
    )(pieces, fixed_block, fixed_load)


def along_col(block, distance):
    return lax.ppermute(block, "col", [(i, (i + distance) % 4) for i in range(4)])


def fixed_body(pat_ref, wg_ref, e_ref, w_ref, b_ref, sums_ref):
    g32 = nn(wg_ref[0], e_ref[0, :S])
    for k in range(1, 4):
        g32 += nn(wg_ref[k], e_ref[0, k * S : (k + 1) * S])
    sums_ref[:64, :64] = nt(g32.astype(BF), w_ref[0])
    over = jnp.int32(0)
    for c in range(4):
        count = jnp.int32(0)
        for kind in range(2):
            for r in range(8):
                for k in range(2):
                    count = count + pat_ref[kind, r, 2 * c + k]
        over = over + (count > SLOTS).astype(jnp.int32)
    sums_ref[:64, 64:] = jnp.full((64, 64), over.astype(F32))
    sums_ref[64:] = lax.dot_general(
        g32, b_ref[0].astype(F32), (((1,), (0,)), ((), ())),
        precision=lax.Precision.HIGHEST, preferred_element_type=F32,
    )


def fixed_terms(pattern, wg, inverse, arrow, rhs):
    return call(
        fixed_body, (1,), 1,
        [full((4, 64, S)), full((1, R, S)), full((1, 64, S)), full((1, S, T))],
        full((128, 128)),
        jax.ShapeDtypeStruct((128, 128), F32),
    )(pattern, wg, inverse, arrow, rhs)


def tile_mask(pattern):
    return jnp.repeat(jnp.repeat(pattern, T, axis=-2), T, axis=-1)


def gathered(array, dim):
    return jnp.concatenate(list(sent_to_all(array, "col")), axis=dim)


def all_tiles(
    inverse, diag, lower, arrow, oarrow, dpattern, pattern, rhs, orhs, x_odd, fixed
):
    col = lax.axis_index("col")
    exists = (lax.axis_index(MONTH) > 0).astype(BF)
    low_odd = gathered(lower[0, 1], 1) * tile_mask(pattern[1]).astype(BF)
    low_prev = gathered(lower[0, 0], 1) * tile_mask(pattern[0]).astype(BF) * exists
    weight = gathered(arrow[0], 1)
    e = inverse[0]
    odd_cols = nn(low_odd, e).astype(BF)
    prev_cols = nn(low_prev, e).astype(BF)
    arrow_cols = nn(weight, e).astype(BF)
    odd_rows = lax.all_to_all(odd_cols, "col", split_axis=0, concat_axis=1, tiled=True)
    prev_rows = lax.all_to_all(prev_cols, "col", split_axis=0, concat_axis=1, tiled=True)
    loads = gathered(rhs[0], 0)
    odd_full = gathered(x_odd[0], 0)
    got = shifted(
        (nt(low_prev, prev_rows), nt(weight, prev_rows), nn(prev_rows, loads)), -1
    )
    prev_full = shifted(odd_full, 1)
    mask = lax.dynamic_slice_in_dim(tile_mask(dpattern).astype(F32), col * S, S, 1)
    rd = diag[0].astype(F32) * mask - nt(low_odd, odd_rows) - got[0]
    rl = -nt(low_odd, prev_rows)
    ra = oarrow[0].astype(F32) - nt(weight, odd_rows) - got[1]
    rr = orhs[0].astype(F32) - nn(odd_rows, loads) - got[2]

    def tn(a, b):
        return lax.dot_general(a, b, (((0,), (0,)), ((), ())), preferred_element_type=F32)

    solved = (
        tn(e, loads) - tn(prev_cols, prev_full) - tn(odd_cols, odd_full)
        - tn(arrow_cols, fixed)
    )
    return rd[None], rl[None], ra[None], rr[None], solved[None]


def per_device(
    even_inverse, odd_diag, lower, arrow, odd_arrow, diag_pattern, lower_pattern,
    rhs, odd_rhs, odd_solution, fixed_block, fixed_load, fixed_solution,
):
    col = lax.axis_index("col")
    month = lax.axis_index(MONTH)
    pos = jnp.stack([col, (month > 0).astype(jnp.int32)]).astype(jnp.int32)
    pattern, dpattern = lower_pattern[0], diag_pattern[0]

    x_prev = shifted(odd_solution, 1)
    wg = sent_to_all(arrow[0], "col")
    to_right, to_left = packed(
        pos, pattern, lower, even_inverse, rhs, odd_solution, x_prev
    )
    to_right, to_left, wg = lax.optimization_barrier((to_right, to_left, wg))
    left = along_col(to_right, 1)
    right = along_col(to_left, -1)
    far_k0 = along_col(left[CUT * T : (SHARE + 2) * T], 1)
    far_k1 = along_col(right[2 * T : (CUT + 4) * T], -1)
    sums = fixed_terms(pattern, wg, even_inverse, arrow, rhs)
    sums = spread(exchanged(sums.reshape(8, 16, 128), MONTH[1:]), 16)
    sums = spread(exchanged(sums, "month_z"), 32)
    sums = exchanged(sums, (*MONTH[1:], "col"))
    reduced_fixed, fixed_rhs, over = settled(sums, fixed_block, fixed_load)
    shares = (to_right, left, right, far_k0, far_k1)
    ahead, v_rows, z = next_terms(pos, pattern, shares, even_inverse, wg)
    got = shifted(ahead, -1)
    here, off, solved = here_terms(
        pos, pattern, shares, even_inverse, wg, v_rows, z, fixed_solution
    )

    def finish():
        rd, ra, rr = reduced_terms(pos, dpattern, here, got, odd_diag, odd_arrow, odd_rhs)
        return rd, off, ra, rr, solved

    def again():
        return all_tiles(
            even_inverse, odd_diag, lower, arrow, odd_arrow, dpattern, pattern,
            rhs, odd_rhs, odd_solution, fixed_solution,
        )

    rd, rl, ra, rr, solved = lax.cond(over[0, 64] > 0.5, again, finish)
    return rd, rl, ra, rr, reduced_fixed, fixed_rhs, solved


def solution(mesh):
    finer = Mesh(
        mesh.devices.reshape(16, 4, 2, mesh.shape["col"]),
        ("month_z", "month_y", "month_k", "col"),
    )
    cols3, rows3 = P(MONTH, None, "col"), P(MONTH, "col", None)
    return jax.shard_map(
        per_device,
        mesh=finer,
        in_specs=(
            cols3, cols3, P(MONTH, None, None, "col"), cols3, cols3,
            P(MONTH, None, None), P(MONTH, None, None, None),
            rows3, rows3, rows3, P(), P(), P(),
        ),
        out_specs=(cols3, cols3, cols3, rows3, P(), P(), rows3),
        check_vma=False,
    )
```

time: 204 us -> 131 us (0.64)
  blocking collectives: 111 us -> 14 us
  Pallas kernels: 0 us -> 27.4 us
  starting transfers between devices: 22.8 us -> 46.7 us
  matrix products: 22.1 us -> 0 us
  waiting for transfers between devices: 12.3 us -> 32.6 us
  between operations: 14.4 us -> 1.57 us
  local copies, waits for them, and re-layouts: 19.5 us -> 7.85 us
    psum x3 -> x0, blocking collectives: 86.3 us -> none  [one_axis_at_a_time(): return functools.reduce(lax.psum, axes, array)]
    pallas_call x0 -> x8, Pallas kernels: none -> 27.4 us  [the longest x1 7.06 us: here_terms(): call(here_body, (1,), 2, SHARE_SPECS + [full((S, R)), full((T, R)), full(...]
    all_gather x2 -> x0, blocking collectives: 24.7 us -> none  [the longest x1 15.1 us: in_one_piece(): out, at, outs = (lax.all_gather(both, axis, axis=dim, tiled=True), 0, [])]
    dot_general x16 -> x0, matrix products: 22.1 us -> none  [the longest x10 16.8 us: contract(): lax.dot_general(left, right, (((left_dim,), (right_dim,)), ((), ())), pre...]
    ppermute x4 -> x6, waiting for transfers between devices: 4.56 us -> 21.3 us  [the longest x4 21.3 us: along_col(): lax.ppermute(block, 'col', [(i, (i + distance) % 4) for i in range(4)])]
    all_to_all x3, starting transfers between devices: 11.7 us -> 26.2 us  [exchanged(): return lax.all_to_all(pieces, axis, split_axis=0, concat_axis=0, tiled=True)]
    all_to_all x0 -> x1, blocking collectives: none -> 14 us  [exchanged(): return lax.all_to_all(pieces, axis, split_axis=0, concat_axis=0, tiled=True)]
    ppermute x4 -> x6, starting transfers between devices: 11 us -> 20.6 us  [the longest x4 12.9 us: along_col(): lax.ppermute(block, 'col', [(i, (i + distance) % 4) for i in range(4)])]
  transfers between devices with their start and end apart: 9 -> 9, of which waited for: 2 -> 4; matrix products, arithmetic and copies ran while one was open for 17% -> 3% of each run, Pallas kernels for 0% -> 19%
where the time goes in v1:
time: 131 us; the launch traced here: 130 us
  starting transfers between devices  46.7 us (36%)
  waiting for transfers between devices  32.6 us (25%)
  Pallas kernels  27.4 us (21%)
  blocking collectives  14 us (11%)
  local copies, waits for them, and re-layouts  7.85 us (6%)
  between operations  1.57 us (1%)
    all_to_all x3, starting transfers between devices, exchanged(): return lax.all_to_all(pieces, axis, split_axis=0, concat_axis=0, tiled=True)  26.2 us
    ppermute x4, waiting for transfers between devices, along_col(): lax.ppermute(block, 'col', [(i, (i + distance) % 4) for i in range(4)])  21.3 us
    all_to_all x1, blocking collectives, exchanged(): return lax.all_to_all(pieces, axis, split_axis=0, concat_axis=0, tiled=True)  14 us
    ppermute x4, starting transfers between devices, along_col(): lax.ppermute(block, 'col', [(i, (i + distance) % 4) for i in range(4)])  12.9 us
    all_to_all x3, waiting for transfers between devices, exchanged(): return lax.all_to_all(pieces, axis, split_axis=0, concat_axis=0, tiled=True)  11.2 us
    ppermute x2, starting transfers between devices, shifted(): return lax.ppermute(block, MONTH, route)  7.67 us
    pallas_call x1, Pallas kernels, here_terms(): call(here_body, (1,), 2, SHARE_SPECS + [full((S, R)), full((T, R)), full(...  7.06 us
    pallas_call x1, Pallas kernels, next_terms(): call(next_body, (1,), 2, SHARE_SPECS, [full((STACK, S)), full((S, R)), fu...  5.97 us
  transfers between devices with their start and end apart: 9, of which 4 were waited for; matrix products, arithmetic and copies ran while one was open for 3% of the time, Pallas kernels for 19%

profile of v1, /device:TPU:1, one launch (start us, length us, event | category | flops | bytes accessed | tf_op | source)
XLA Modules:
  0.0 130.2 jit_solution(5929752466829385647)
XLA Ops:
  0.7 4.7 %collective-permute-start.4 = (bf16[1,256,128]{2,1,0:T(8,128)(2,1)}, bf16[1,256,128]{2,1,0:T(8,128)(2,1)S(1)}, u32[]{:S(2)}, u32[]{:S(2)}) collective-permute-start(bf16[1,256,128]{2,1,0:T(8,128)(2,1)} %x_ref.1), channel_id=1, source_target_pairs={{0,4},{4,8},{8,12},{12,16},{16,20},{20,24},{24,28},{28,32},{32,36}... | collective-permute-start | bytes 196616 | tf_op jit(solution)/shard_map/ppermute | solution.py:27
  5.4 1.4 %broadcast_in_dim.51 = bf16[4,64,256]{2,1,0:T(8,128)(2,1)} broadcast(bf16[64,256]{1,0:T(8,128)(2,1)} %bitcast.143), dimensions={1,2} | broadcast | bytes 163840 | tf_op jit(solution)/shard_map/broadcast_in_dim | solution.py:35
  6.8 4.0 %all-to-all-start.7 = ((bf16[4,64,256]{2,1,0:T(8,128)(2,1)}), bf16[4,64,256]{2,1,0:T(8,128)(2,1)S(1)}, u32[]{:S(2)}, u32[]{:S(2)}) async-start(bf16[4,64,256]{2,1,0:T(8,128)(2,1)} %broadcast_in_dim.51), calls=%async_computation.7 | async-start | bytes 262144 | tf_op jit(solution)/shard_map/all_to_all | solution.py:31
  10.8 0.1 pad_add_fusion.pos_ref
  10.9 0.6 copy-done.34
  11.5 4.0 %shard_map.180 = (bf16[3840,128]{1,0:T(8,128)(2,1)}, bf16[4352,128]{1,0:T(8,128)(2,1)}) custom-call(s32[2]{0:T(128)S(1)} %pad_add_fusion.pos_ref, s32[2,8,8]{2,1,0:T(8,128)} %bitcast.147, bf16[1,2,1024,256]{3,2,1,0:T(8,128)(2,1)} %low_ref.1, bf16[1,1024,256]{2,1,0:T(8,128)(2,1)} %refs_5_.3, bf16[1,256,128]{2,1,0:T(8,128)(2,1)} %b_ref.3, ...), custom_call_target="tpu_custom_call" | custom-call | tf_op jit(solution)/shard_map/pallas_call | solution.py:103
  15.7 4.5 %collective-permute-start.6 = (bf16[4352,128]{1,0:T(8,128)(2,1)}, bf16[4352,128]{1,0:T(8,128)(2,1)S(1)}, u32[]{:S(2)}, u32[]{:S(2)}) collective-permute-start(bf16[4352,128]{1,0:T(8,128)(2,1)} %get-tuple-element.94), channel_id=1, source_target_pairs={{0,3},{1,0},{2,1},{3,2},{4,7},{5,4},{6,5},{7,6},{8,11},{9,8},{10,9... | collective-permute-start | bytes 3342344 | tf_op jit(solution)/shard_map/ppermute | solution.py:347
  20.2 1.9 %collective-permute-start.5 = (bf16[3840,128]{1,0:T(8,128)(2,1)}, bf16[3840,128]{1,0:T(8,128)(2,1)S(1)}, u32[]{:S(2)}, u32[]{:S(2)}) collective-permute-start(bf16[3840,128]{1,0:T(8,128)(2,1)} %get-tuple-element.93.refs_0_), channel_id=1, source_target_pairs={{0,1},{1,2},{2,3},{3,0},{4,5},{5,6},{6,7},{7,4},{8,9},{9,10},{10,1... | collective-permute-start | bytes 2949128 | tf_op jit(solution)/shard_map/ppermute | solution.py:347
  22.1 21.3 %collective-permute-done.5.refs_1_ = bf16[3840,128]{1,0:T(8,128)(2,1)S(1)} collective-permute-done((bf16[3840,128]{1,0:T(8,128)(2,1)}, bf16[3840,128]{1,0:T(8,128)(2,1)S(1)}, u32[]{:S(2)}, u32[]{:S(2)}) %collective-permute-start.5) | collective-permute-done | bytes 983072 | tf_op jit(solution)/shard_map/ppermute | solution.py:347
  43.4 0.9 slice.28
  44.3 1.9 %collective-permute-start.7 = (bf16[1920,128]{1,0:T(8,128)(2,1)}, bf16[1920,128]{1,0:T(8,128)(2,1)S(1)}, u32[]{:S(2)}, u32[]{:S(2)}) collective-permute-start(bf16[1920,128]{1,0:T(8,128)(2,1)} %slice.28), channel_id=1, source_target_pairs={{0,1},{1,2},{2,3},{3,0},{4,5},{5,6},{6,7},{7,4},{8,9},{9,10},{10,1... | collective-permute-start | bytes 1474568 | tf_op jit(solution)/shard_map/ppermute | solution.py:347
  46.2 0.8 slice.29
  47.0 4.6 %collective-permute-start.8 = (bf16[1408,128]{1,0:T(8,128)(2,1)}, bf16[1408,128]{1,0:T(8,128)(2,1)}, u32[]{:S(2)}, u32[]{:S(2)}) collective-permute-start(bf16[1408,128]{1,0:T(8,128)(2,1)} %slice.29), channel_id=1, source_target_pairs={{0,3},{1,0},{2,1},{3,2},{4,7},{5,4},{6,5},{7,6},{8,11},{9,8},{10,9... | collective-permute-start | bytes 1081352 | tf_op jit(solution)/shard_map/ppermute | solution.py:347
  51.6 2.7 %shard_map.181 = f32[128,128]{1,0:T(8,128)} custom-call(s32[2,8,8]{2,1,0:T(8,128)S(1)} %bitcast.148, bf16[4,64,256]{2,1,0:T(8,128)(2,1)} %copy-done.4, bf16[1,1024,256]{2,1,0:T(8,128)(2,1)S(1)} %copy-done, bf16[1,64,256]{2,1,0:T(8,128)(2,1)S(1)} %copy-done.17, bf16[1,256,128]{2,1,0:T(8,128)(2,1)S(1)} %copy-done.13), custom_call_target="tpu_custom_call" | custom-call | tf_op jit(solution)/shard_map/pallas_call | solution.py:371
  54.3 14.0 %all_to_all.72.pieces_ref = f32[8,16,128]{2,1,0:T(8,128)} all-to-all(f32[8,16,128]{2,1,0:T(8,128)} %bitcast.145), channel_id=1, replica_groups=mesh['month_z'=16,'month_y'=4,'month_k'=2,'col'=4] {'month_y','month_k'}, dimensions={0} | all-to-all | bytes 131072 | tf_op jit(solution)/shard_map/all_to_all | solution.py:31
  68.4 1.5 %shard_map.182 = f32[16,16,128]{2,1,0:T(8,128)} custom-call(f32[8,16,128]{2,1,0:T(8,128)} %all_to_all.72.pieces_ref), custom_call_target="tpu_custom_call" | custom-call | tf_op jit(solution)/shard_map/pallas_call | solution.py:312
  69.9 14.8 %all-to-all-start.9 = ((f32[16,16,128]{2,1,0:T(8,128)}), f32[16,16,128]{2,1,0:T(8,128)S(1)}, u32[]{:S(2)}, u32[]{:S(2)}) async-start(f32[16,16,128]{2,1,0:T(8,128)} %shard_map.182), calls=%async_computation.9 | async-start | bytes 262144 | tf_op jit(solution)/shard_map/all_to_all | solution.py:31
  84.7 0.8 copy-done.11
  85.5 6.0 %shard_map.185 = (bf16[1216,256]{1,0:T(8,128)(2,1)}, bf16[256,1024]{1,0:T(8,128)(2,1)}, f32[128,1024]{1,0:T(8,128)}) custom-call(s32[2]{0:T(128)S(1)} %pad_add_fusion.pos_ref, s32[2,8,8]{2,1,0:T(8,128)S(1)} %bitcast.149, bf16[3840,128]{1,0:T(8,128)(2,1)} %get-tuple-element.93.refs_0_, bf16[3840,128]{1,0:T(8,128)(2,1)} %copy-done.1, ...), custom_call_target="tpu_custom_call" | custom-call | tf_op jit(solution)/shard_map/pallas_call | solution.py:220
  91.5 3.0 %collective-permute-start.9 = (bf16[1216,256]{1,0:T(8,128)(2,1)}, bf16[1216,256]{1,0:T(8,128)(2,1)}, u32[]{:S(2)}, u32[]{:S(2)}) collective-permute-start(bf16[1216,256]{1,0:T(8,128)(2,1)} %get-tuple-element.98), channel_id=1, source_target_pairs={{4,0},{8,4},{12,8},{16,12},{20,16},{24,20},{28,24},{32,28},{36,32}... | collective-permute-start | bytes 1867784 | tf_op jit(solution)/shard_map/ppermute | solution.py:27
  94.4 2.2 %all-to-all-done.9.pieces_ref = f32[16,16,128]{2,1,0:T(8,128)S(1)} async-done(((f32[16,16,128]{2,1,0:T(8,128)}), f32[16,16,128]{2,1,0:T(8,128)S(1)}, u32[]{:S(2)}, u32[]{:S(2)}) %all-to-all-start.9) | async-done | bytes 131104 | tf_op jit(solution)/shard_map/all_to_all | solution.py:31
  96.7 0.7 copy-done.14
  97.3 1.6 %shard_map.183 = f32[32,16,128]{2,1,0:T(8,128)} custom-call(f32[16,16,128]{2,1,0:T(8,128)} %copy-done.14), custom_call_target="tpu_custom_call" | custom-call | tf_op jit(solution)/shard_map/pallas_call | solution.py:312
  98.9 7.4 %all-to-all-start.10 = ((f32[32,16,128]{2,1,0:T(8,128)}), f32[32,16,128]{2,1,0:T(8,128)S(1)}, u32[]{:S(2)}, u32[]{:S(2)}) async-start(f32[32,16,128]{2,1,0:T(8,128)} %shard_map.183), calls=%async_computation.10 | async-start | bytes 524288 | tf_op jit(solution)/shard_map/all_to_all | solution.py:31
  106.3 9.0 %all-to-all-done.10.pieces_ref = f32[32,16,128]{2,1,0:T(8,128)S(1)} async-done(((f32[32,16,128]{2,1,0:T(8,128)}), f32[32,16,128]{2,1,0:T(8,128)S(1)}, u32[]{:S(2)}, u32[]{:S(2)}) %all-to-all-start.10) | async-done | bytes 262176 | tf_op jit(solution)/shard_map/all_to_all | solution.py:31
  115.3 0.7 copy-done.12
  116.0 1.6 %shard_map.184 = (f32[64,64]{1,0:T(8,128)}, f32[64,128]{1,0:T(8,128)}, f32[8,128]{1,0:T(8,128)}) custom-call(f32[32,16,128]{2,1,0:T(8,128)} %copy-done.12, f32[64,64]{1,0:T(8,128)} %block_ref.1, f32[64,128]{1,0:T(8,128)} %load_ref.1), custom_call_target="tpu_custom_call" | custom-call | tf_op jit(solution)/shard_map/pallas_call | solution.py:334
  117.6 1.3 slice.23
  119.6 7.1 %shard_map.186 = (f32[1216,256]{1,0:T(8,128)S(1)}, f32[1,1024,256]{2,1,0:T(8,128)}, f32[1,256,128]{2,1,0:T(8,128)}) custom-call(s32[2]{0:T(128)S(1)} %pad_add_fusion.pos_ref, s32[2,8,8]{2,1,0:T(8,128)S(1)} %bitcast.150, bf16[3840,128]{1,0:T(8,128)(2,1)} %get-tuple-element.93.refs_0_, bf16[3840,128]{1,0:T(8,128)(2,1)} %copy-done.1, ...), custom_call_target="tpu_custom_call" | custom-call | tf_op jit(solution)/shard_map/pallas_call | solution.py:257
  126.7 2.9 %conditional.1 = (f32[1,1024,256]{2,1,0:T(8,128)}, f32[1,1024,256]{2,1,0:T(8,128)}, f32[1,64,256]{2,1,0:T(8,128)}, f32[1,256,128]{2,1,0:T(8,128)S(1)}, f32[1,256,128]{2,1,0:T(8,128)}) conditional(s32[]{:T(128)} %bitcast.45, (s32[2]{0:T(128)S(1)}, s32[8,8]{1,0:T(8,128)S(1)}, f32[1216,256]{1,0:T(8,128)S(1)}, bf16[1216,256]{1,0:T(8,128)(2,1)}, ...), branch_computations={%region_0.0_spmd, %region_1.0_spmd} | conditional | flops 3156738304 | bytes 125719288 | solution.py:464
  126.7 2.9 %branch_0_fun.1 = (f32[1,1024,256]{2,1,0:T(8,128)}, f32[1,64,256]{2,1,0:T(8,128)}, f32[1,256,128]{2,1,0:T(8,128)S(1)}) custom-call(s32[2]{0:T(128)S(1)} %get-tuple-element.40.pos_ref, s32[8,8]{1,0:T(8,128)S(1)} %get-tuple-element.41.dpat_ref, f32[1216,256]{1,0:T(8,128)S(1)} %get-tuple-element.42.here_ref, bf16[1216,256]{1,0:T(8,128)(2,1)} %get-tuple-element.43.got_ref, ...), custom_call_target="tpu_custom_call" | custom-call | tf_op jit(solution)/shard_map/cond/branch_0_fun/pallas_call | solution.py:287
  129.6 0.7 copy-done.47
  (35 shorter events, 0.2 us)
Async XLA Ops:
  0.6 51.0 %copy-start.17 = (bf16[1,64,256]{2,1,0:T(8,128)(2,1)S(1)}, bf16[1,64,256]{2,1,0:T(8,128)(2,1)}, u32[]{:S(2)}) copy-start(bf16[1,64,256]{2,1,0:T(8,128)(2,1)} %w_ref.1) | copy-start | bytes 98308
  0.6 51.0 %copy-start = (bf16[1,1024,256]{2,1,0:T(8,128)(2,1)S(1)}, bf16[1,1024,256]{2,1,0:T(8,128)(2,1)}, u32[]{:S(2)}) copy-start(bf16[1,1024,256]{2,1,0:T(8,128)(2,1)} %refs_5_.3) | copy-start | bytes 1572868
  0.7 51.0 %copy-start.13 = (bf16[1,256,128]{2,1,0:T(8,128)(2,1)S(1)}, bf16[1,256,128]{2,1,0:T(8,128)(2,1)}, u32[]{:S(2)}) copy-start(bf16[1,256,128]{2,1,0:T(8,128)(2,1)} %b_ref.3) | copy-start | bytes 196612
  0.7 51.0 %copy-start.23 = (s32[1,2,8,8]{3,2,1,0:T(8,128)S(1)}, s32[1,2,8,8]{3,2,1,0:T(8,128)}, u32[]{:S(2)}) copy-start(s32[1,2,8,8]{3,2,1,0:T(8,128)} %param.21) | copy-start | bytes 1540
  0.7 10.2 %collective-permute-start.4 = (bf16[1,256,128]{2,1,0:T(8,128)(2,1)}, bf16[1,256,128]{2,1,0:T(8,128)(2,1)S(1)}, u32[]{:S(2)}, u32[]{:S(2)}) collective-permute-start(bf16[1,256,128]{2,1,0:T(8,128)(2,1)} %x_ref.1), channel_id=1, source_target_pairs={{0,4},{4,8},{8,12},{12,16},{16,20},{20,24},{24,28},{28,32},{32,36}... | collective-permute-start | bytes 196616 | tf_op jit(solution)/shard_map/ppermute | solution.py:27
  6.8 8.8 %all-to-all-start.7 = ((bf16[4,64,256]{2,1,0:T(8,128)(2,1)}), bf16[4,64,256]{2,1,0:T(8,128)(2,1)S(1)}, u32[]{:S(2)}, u32[]{:S(2)}) async-start(bf16[4,64,256]{2,1,0:T(8,128)(2,1)} %broadcast_in_dim.51), calls=%async_computation.7 | async-start | bytes 262144 | tf_op jit(solution)/shard_map/all_to_all | solution.py:31
  10.9 0.6 copy-start.34
  15.7 35.9 %copy-start.4 = (bf16[4,64,256]{2,1,0:T(8,128)(2,1)}, bf16[4,64,256]{2,1,0:T(8,128)(2,1)S(1)}, u32[]{:S(2)}) copy-start(bf16[4,64,256]{2,1,0:T(8,128)(2,1)S(1)} %all-to-all-done.7.wg_ref.refs_6_) | copy-start | bytes 393220
  15.7 30.5 %collective-permute-start.6 = (bf16[4352,128]{1,0:T(8,128)(2,1)}, bf16[4352,128]{1,0:T(8,128)(2,1)S(1)}, u32[]{:S(2)}, u32[]{:S(2)}) collective-permute-start(bf16[4352,128]{1,0:T(8,128)(2,1)} %get-tuple-element.94), channel_id=1, source_target_pairs={{0,3},{1,0},{2,1},{3,2},{4,7},{5,4},{6,5},{7,6},{8,11},{9,8},{10,9... | collective-permute-start | bytes 3342344 | tf_op jit(solution)/shard_map/ppermute | solution.py:347
  20.2 23.2 %collective-permute-start.5 = (bf16[3840,128]{1,0:T(8,128)(2,1)}, bf16[3840,128]{1,0:T(8,128)(2,1)S(1)}, u32[]{:S(2)}, u32[]{:S(2)}) collective-permute-start(bf16[3840,128]{1,0:T(8,128)(2,1)} %get-tuple-element.93.refs_0_), channel_id=1, source_target_pairs={{0,1},{1,2},{2,3},{3,0},{4,5},{5,6},{6,7},{7,4},{8,9},{9,10},{10,1... | collective-permute-start | bytes 2949128 | tf_op jit(solution)/shard_map/ppermute | solution.py:347
  43.4 41.3 %copy-start.1 = (bf16[3840,128]{1,0:T(8,128)(2,1)}, bf16[3840,128]{1,0:T(8,128)(2,1)S(1)}, u32[]{:S(2)}) copy-start(bf16[3840,128]{1,0:T(8,128)(2,1)S(1)} %collective-permute-done.5.refs_1_) | copy-start | bytes 2949124
  44.3 40.4 %collective-permute-start.7 = (bf16[1920,128]{1,0:T(8,128)(2,1)}, bf16[1920,128]{1,0:T(8,128)(2,1)S(1)}, u32[]{:S(2)}, u32[]{:S(2)}) collective-permute-start(bf16[1920,128]{1,0:T(8,128)(2,1)} %slice.28), channel_id=1, source_target_pairs={{0,1},{1,2},{2,3},{3,0},{4,5},{5,6},{6,7},{7,4},{8,9},{9,10},{10,1... | collective-permute-start | bytes 1474568 | tf_op jit(solution)/shard_map/ppermute | solution.py:347
  46.2 38.5 %copy-start.2 = (bf16[4352,128]{1,0:T(8,128)(2,1)}, bf16[4352,128]{1,0:T(8,128)(2,1)S(1)}, u32[]{:S(2)}) copy-start(bf16[4352,128]{1,0:T(8,128)(2,1)S(1)} %collective-permute-done.6.refs_2_) | copy-start | bytes 3342340
  47.0 37.7 %collective-permute-start.8 = (bf16[1408,128]{1,0:T(8,128)(2,1)}, bf16[1408,128]{1,0:T(8,128)(2,1)}, u32[]{:S(2)}, u32[]{:S(2)}) collective-permute-start(bf16[1408,128]{1,0:T(8,128)(2,1)} %slice.29), channel_id=1, source_target_pairs={{0,3},{1,0},{2,1},{3,2},{4,7},{5,4},{6,5},{7,6},{8,11},{9,8},{10,9... | collective-permute-start | bytes 1081352 | tf_op jit(solution)/shard_map/ppermute | solution.py:347
  69.9 26.8 %all-to-all-start.9 = ((f32[16,16,128]{2,1,0:T(8,128)}), f32[16,16,128]{2,1,0:T(8,128)S(1)}, u32[]{:S(2)}, u32[]{:S(2)}) async-start(f32[16,16,128]{2,1,0:T(8,128)} %shard_map.182), calls=%async_computation.9 | async-start | bytes 262144 | tf_op jit(solution)/shard_map/all_to_all | solution.py:31
  84.7 0.8 copy-start.11
  91.5 35.2 %collective-permute-start.9 = (bf16[1216,256]{1,0:T(8,128)(2,1)}, bf16[1216,256]{1,0:T(8,128)(2,1)}, u32[]{:S(2)}, u32[]{:S(2)}) collective-permute-start(bf16[1216,256]{1,0:T(8,128)(2,1)} %get-tuple-element.98), channel_id=1, source_target_pairs={{4,0},{8,4},{12,8},{16,12},{20,16},{24,20},{28,24},{32,28},{36,32}... | collective-permute-start | bytes 1867784 | tf_op jit(solution)/shard_map/ppermute | solution.py:27
  96.6 0.7 copy-start.14
  98.9 16.3 %all-to-all-start.10 = ((f32[32,16,128]{2,1,0:T(8,128)}), f32[32,16,128]{2,1,0:T(8,128)S(1)}, u32[]{:S(2)}, u32[]{:S(2)}) async-start(f32[32,16,128]{2,1,0:T(8,128)} %shard_map.183), calls=%async_computation.10 | async-start | bytes 524288 | tf_op jit(solution)/shard_map/all_to_all | solution.py:31
  115.3 0.7 copy-start.12
  119.5 7.1 %copy-start.3 = (bf16[1,2,1024,256]{3,2,1,0:T(8,128)(2,1)S(1)}, bf16[1,2,1024,256]{3,2,1,0:T(8,128)(2,1)}, u32[]{:S(2)}) copy-start(bf16[1,2,1024,256]{3,2,1,0:T(8,128)(2,1)} %low_ref.1) | copy-start | bytes 3145732
  119.5 7.1 %copy-start.6 = (bf16[1,1024,256]{2,1,0:T(8,128)(2,1)S(1)}, bf16[1,1024,256]{2,1,0:T(8,128)(2,1)}, u32[]{:S(2)}) copy-start(bf16[1,1024,256]{2,1,0:T(8,128)(2,1)} %param.16) | copy-start | bytes 1572868
  119.5 7.1 %copy-start.18 = (bf16[1,256,128]{2,1,0:T(8,128)(2,1)S(1)}, bf16[1,256,128]{2,1,0:T(8,128)(2,1)}, u32[]{:S(2)}) copy-start(bf16[1,256,128]{2,1,0:T(8,128)(2,1)} %x_ref.1) | copy-start | bytes 196612
  119.5 7.1 %copy-start.35 = (bf16[1,64,256]{2,1,0:T(8,128)(2,1)S(1)}, bf16[1,64,256]{2,1,0:T(8,128)(2,1)}, u32[]{:S(2)}) copy-start(bf16[1,64,256]{2,1,0:T(8,128)(2,1)} %param.19) | copy-start | bytes 98308
  119.6 7.1 %copy-start.43 = (s32[1,8,8]{2,1,0:T(8,128)S(1)}, s32[1,8,8]{2,1,0:T(8,128)}, u32[]{:S(2)}) copy-start(s32[1,8,8]{2,1,0:T(8,128)} %param.20) | copy-start | bytes 772
  129.6 0.7 copy-start.47

commit v2 on v1

--- a/solution.py
+++ b/solution.py
@@ -15,10 +15,11 @@
 R = 1024
 SLOTS = 16
 SHARE = SLOTS + 6
-CUT = 9
+CUT = 11
 TO_RIGHT = SHARE + 8
 TO_LEFT = SHARE + 12
 STACK = R + T + 64
+VMEM_LIMIT = 20 * 1024 * 1024
 
 
 def shifted(block, distance):
@@ -43,8 +44,8 @@
     return lax.dot_general(a, b, (((1,), (1,)), ((), ())), preferred_element_type=F32)
 
 
-def full(shape):
-    return pl.BlockSpec(shape, lambda *_: (0,) * len(shape))
+def full():
+    return pl.BlockSpec(memory_space=pltpu.VMEM)
 
 
 def flipped(x):
@@ -62,6 +63,7 @@
             scratch_shapes=list(scratch),
         ),
         out_shape=out_shape,
+        compiler_params=pltpu.CompilerParams(vmem_limit_bytes=VMEM_LIMIT),
     )
 
 
@@ -101,9 +103,9 @@
 
 def packed(pos, pattern, lower, inverse, rhs, x_odd, x_prev):
     return call(
-        pack_body, (1,), 2,
-        [full((1, 2, R, S)), full((1, R, S))] + [full((1, S, T))] * 3,
-        [full((TO_RIGHT * T, T)), full((TO_LEFT * T, T))],
+        pack_body, (), 2,
+        [full(), full()] + [full()] * 3,
+        [full(), full()],
         (
             jax.ShapeDtypeStruct((TO_RIGHT * T, T), BF),
             jax.ShapeDtypeStruct((TO_LEFT * T, T), BF),
@@ -198,9 +200,9 @@
 
 
 SHARE_SPECS = [
-    full((TO_RIGHT * T, T)), full((TO_RIGHT * T, T)), full((TO_LEFT * T, T)),
-    full(((SHARE - CUT + 2) * T, T)), full(((CUT + 2) * T, T)),
-    full((1, R, S)), full((4, 64, S)),
+    full(), full(), full(),
+    full(), full(),
+    full(), full(),
 ]
 SHARE_SCRATCH = [pltpu.VMEM((SHARE * T, T), BF), pltpu.VMEM((STACK, R), BF)]
 
@@ -218,8 +220,8 @@
 
 def next_terms(pos, pattern, shares, inverse, wg):
     return call(
-        next_body, (1,), 2, SHARE_SPECS,
-        [full((STACK, S)), full((S, R)), full((T, R))],
+        next_body, (), 2, SHARE_SPECS,
+        [full(), full(), full()],
         (
             jax.ShapeDtypeStruct((STACK, S), BF),
             jax.ShapeDtypeStruct((S, R), BF),
@@ -255,9 +257,9 @@
 
 def here_terms(pos, pattern, shares, inverse, wg, v_rows, z, fixed):
     return call(
-        here_body, (1,), 2,
-        SHARE_SPECS + [full((S, R)), full((T, R)), full((64, T))],
-        [full((STACK, S)), full((1, R, S)), full((1, S, T))],
+        here_body, (), 2,
+        SHARE_SPECS + [full(), full(), full()],
+        [full(), full(), full()],
         (
             jax.ShapeDtypeStruct((STACK, S), F32),
             jax.ShapeDtypeStruct((1, R, S), F32),
@@ -285,12 +287,12 @@
 
 def reduced_terms(pos, dpattern, here, got, diag, oarrow, orhs):
     return call(
-        reduced_body, (1,), 2,
+        reduced_body, (), 2,
         [
-            full((STACK, S)), full((STACK, S)), full((1, R, S)),
-            full((1, 64, S)), full((1, S, T)),
+            full(), full(), full(),
+            full(), full(),
         ],
-        [full((1, R, S)), full((1, 64, S)), full((1, S, T))],
+        [full(), full(), full()],
         (
             jax.ShapeDtypeStruct((1, R, S), F32),
             jax.ShapeDtypeStruct((1, 64, S), F32),
@@ -310,7 +312,7 @@
 def spread(pieces, copies):
     shape = pieces.shape[1:]
     return call(
-        spread_body, (1,), 0, [full(pieces.shape)], full((copies, *shape)),
+        spread_body, (), 0, [full()], full(),
         jax.ShapeDtypeStruct((copies, *shape), F32),
     )(pieces)
 
@@ -327,18 +329,21 @@
             rows = slice(16 * n - 64, 16 * n - 48)
             rhs_ref[rows] = load_ref[rows] - total
         if n == 0:
-            over_ref[...] = total[:8]
+            over_ref[0, 0] = jnp.max(total[:8, 64:]).astype(jnp.int32)
 
 
 def settled(pieces, fixed_block, fixed_load):
     return call(
-        settle_body, (1,), 0,
-        [full((32, 16, 128)), full((64, 64)), full((64, 128))],
-        [full((64, 64)), full((64, 128)), full((8, 128))],
+        settle_body, (), 0,
+        [full(), full(), full()],
+        [
+            full(), full(),
+            pl.BlockSpec(memory_space=pltpu.SMEM),
+        ],
         (
             jax.ShapeDtypeStruct((64, 64), F32),
             jax.ShapeDtypeStruct((64, 128), F32),
-            jax.ShapeDtypeStruct((8, 128), F32),
+            jax.ShapeDtypeStruct((1, 1), jnp.int32),
         ),
     )(pieces, fixed_block, fixed_load)
 
@@ -369,9 +374,9 @@
 
 def fixed_terms(pattern, wg, inverse, arrow, rhs):
     return call(
-        fixed_body, (1,), 1,
-        [full((4, 64, S)), full((1, R, S)), full((1, 64, S)), full((1, S, T))],
-        full((128, 128)),
+        fixed_body, (), 1,
+        [full(), full(), full(), full()],
+        full(),
         jax.ShapeDtypeStruct((128, 128), F32),
     )(pattern, wg, inverse, arrow, rhs)
 
@@ -434,7 +439,6 @@
     to_right, to_left = packed(
         pos, pattern, lower, even_inverse, rhs, odd_solution, x_prev
     )
-    to_right, to_left, wg = lax.optimization_barrier((to_right, to_left, wg))
     left = along_col(to_right, 1)
     right = along_col(to_left, -1)
     far_k0 = along_col(left[CUT * T : (SHARE + 2) * T], 1)
@@ -461,7 +465,7 @@
             rhs, odd_rhs, odd_solution, fixed_solution,
         )
 
-    rd, rl, ra, rr, solved = lax.cond(over[0, 64] > 0.5, again, finish)
+    rd, rl, ra, rr, solved = lax.cond(over[0, 0] > 0, again, finish)
     return rd, rl, ra, rr, reduced_fixed, fixed_rhs, solved
 
 

time: 131 us -> 129 us (0.985)
  Pallas kernels: 27.4 us -> 17.6 us
  waiting for transfers between devices: 32.6 us -> 38.6 us
  blocking collectives: 14 us -> 18.9 us
  starting transfers between devices: 46.7 us -> 43.6 us
    pallas_call x8, Pallas kernels: 27.4 us -> 17.6 us  [the longest x1 5.24 us: here_terms(): call(here_body, (), 2, SHARE_SPECS + [full(), full(), full()], [full(), f...]
    all_to_all x1 -> x2, blocking collectives: 14 us -> 18.9 us  [exchanged(): return lax.all_to_all(pieces, axis, split_axis=0, concat_axis=0, tiled=True)]
    ppermute x2, waiting for transfers between devices: 0.01 us -> 4.39 us  [shifted(): return lax.ppermute(block, MONTH, route)]
    unnamed x34 -> x44, local copies, waits for them, and re-layouts: 3.49 us -> 5.82 us
    all_to_all x3 -> x2, starting transfers between devices: 26.2 us -> 24.2 us  [exchanged(): return lax.all_to_all(pieces, axis, split_axis=0, concat_axis=0, tiled=True)]
    ppermute x4, waiting for transfers between devices: 21.3 us -> 23 us  [along_col(): lax.ppermute(block, 'col', [(i, (i + distance) % 4) for i in range(4)])]
    broadcast_in_dim x1, local copies, waits for them, and re-layouts: 1.42 us -> 0.01 us  [sent_to_all(): jnp.broadcast_to(array, (lax.axis_size(axis), *array.shape))]
    all_to_all x3 -> x2, waiting for transfers between devices: 11.2 us -> 11.2 us  [exchanged(): return lax.all_to_all(pieces, axis, split_axis=0, concat_axis=0, tiled=True)]
  transfers between devices with their start and end apart: 9 -> 8, of which waited for: 4 -> 4; matrix products, arithmetic and copies ran while one was open for 3% -> 1% of each run, Pallas kernels for 19% -> 10%
where the time goes in v2:
time: 129 us; the launch traced here: 128 us
  starting transfers between devices  43.6 us (34%)
  waiting for transfers between devices  38.6 us (30%)
  blocking collectives  18.9 us (15%)
  Pallas kernels  17.6 us (14%)
  local copies, waits for them, and re-layouts  7.4 us (6%)
  between operations  1.63 us (1%)
    all_to_all x2, starting transfers between devices, exchanged(): return lax.all_to_all(pieces, axis, split_axis=0, concat_axis=0, tiled=True)  24.2 us
    ppermute x4, waiting for transfers between devices, along_col(): lax.ppermute(block, 'col', [(i, (i + distance) % 4) for i in range(4)])  23 us
    all_to_all x2, blocking collectives, exchanged(): return lax.all_to_all(pieces, axis, split_axis=0, concat_axis=0, tiled=True)  18.9 us
    ppermute x4, starting transfers between devices, along_col(): lax.ppermute(block, 'col', [(i, (i + distance) % 4) for i in range(4)])  11.8 us
    all_to_all x2, waiting for transfers between devices, exchanged(): return lax.all_to_all(pieces, axis, split_axis=0, concat_axis=0, tiled=True)  11.2 us
    ppermute x2, starting transfers between devices, shifted(): return lax.ppermute(block, MONTH, route)  7.68 us
    unnamed x44, local copies, waits for them, and re-layouts  5.82 us
    pallas_call x1, Pallas kernels, here_terms(): call(here_body, (), 2, SHARE_SPECS + [full(), full(), full()], [full(), f...  5.24 us
  transfers between devices with their start and end apart: 8, of which 4 were waited for; matrix products, arithmetic and copies ran while one was open for 1% of the time, Pallas kernels for 10%

profile of v2, /device:TPU:1, one launch (start us, length us, event | category | flops | bytes accessed | tf_op | source)
XLA Modules:
  0.0 128.0 jit_solution(10680039955154983566)
XLA Ops:
  0.7 4.7 %collective-permute-start.4 = (bf16[1,256,128]{2,1,0:T(8,128)(2,1)}, bf16[1,256,128]{2,1,0:T(8,128)(2,1)S(1)}, u32[]{:S(2)}, u32[]{:S(2)}) collective-permute-start(bf16[1,256,128]{2,1,0:T(8,128)(2,1)} %x_ref.1), channel_id=1, source_target_pairs={{0,4},{4,8},{8,12},{12,16},{16,20},{20,24},{24,28},{28,32},{32,36}... | collective-permute-start | bytes 196616 | tf_op jit(solution)/shard_map/ppermute | solution.py:28
  5.4 0.1 pad_add_fusion.pos_ref
  5.5 4.4 %collective-permute-done.4.xp_ref = bf16[1,256,128]{2,1,0:T(8,128)(2,1)S(1)} collective-permute-done((bf16[1,256,128]{2,1,0:T(8,128)(2,1)}, bf16[1,256,128]{2,1,0:T(8,128)(2,1)S(1)}, u32[]{:S(2)}, u32[]{:S(2)}) %collective-permute-start.4) | collective-permute-done | bytes 65568 | tf_op jit(solution)/shard_map/ppermute | solution.py:28
  9.9 2.7 %shard_map.184 = (bf16[3840,128]{1,0:T(8,128)(2,1)S(1)}, bf16[4352,128]{1,0:T(8,128)(2,1)S(1)}) custom-call(s32[2]{0:T(128)S(1)} %pad_add_fusion.pos_ref, s32[2,8,8]{2,1,0:T(8,128)} %bitcast.147, bf16[1,2,1024,256]{3,2,1,0:T(8,128)(2,1)} %low_ref.1, bf16[1,1024,256]{2,1,0:T(8,128)(2,1)} %refs_5_.3, bf16[1,256,128]{2,1,0:T(8,128)(2,1)} %b_ref.3, ...), custom_call_target="tpu_custom_call" | custom-call | tf_op jit(solution)/shard_map/pallas_call | solution.py:105
  12.6 1.9 %collective-permute-start.6 = (bf16[4352,128]{1,0:T(8,128)(2,1)S(1)}, bf16[4352,128]{1,0:T(8,128)(2,1)S(1)}, u32[]{:S(2)}, u32[]{:S(2)}) collective-permute-start(bf16[4352,128]{1,0:T(8,128)(2,1)S(1)} %get-tuple-element.88), channel_id=1, source_target_pairs={{0,3},{1,0},{2,1},{3,2},{4,7},{5,4},{6,5},{7,6},{8,11},{9,8},{10,9... | collective-permute-start | bytes 3342344 | tf_op jit(solution)/shard_map/ppermute | solution.py:352
  14.5 3.4 %collective-permute-start.5 = (bf16[3840,128]{1,0:T(8,128)(2,1)S(1)}, bf16[3840,128]{1,0:T(8,128)(2,1)S(1)}, u32[]{:S(2)}, u32[]{:S(2)}) collective-permute-start(bf16[3840,128]{1,0:T(8,128)(2,1)S(1)} %get-tuple-element.87.refs_0_), channel_id=1, source_target_pairs={{0,1},{1,2},{2,3},{3,0},{4,5},{5,6},{6,7},{7,4},{8,9},{9,10},{10,1... | collective-permute-start | bytes 2949128 | tf_op jit(solution)/shard_map/ppermute | solution.py:352
  17.9 22.9 %collective-permute-done.5.refs_1_ = bf16[3840,128]{1,0:T(8,128)(2,1)S(1)} collective-permute-done((bf16[3840,128]{1,0:T(8,128)(2,1)S(1)}, bf16[3840,128]{1,0:T(8,128)(2,1)S(1)}, u32[]{:S(2)}, u32[]{:S(2)}) %collective-permute-start.5) | collective-permute-done | bytes 983072 | tf_op jit(solution)/shard_map/ppermute | solution.py:352
  40.8 0.8 slice.24
  41.6 1.9 %collective-permute-start.7 = (bf16[1664,128]{1,0:T(8,128)(2,1)}, bf16[1664,128]{1,0:T(8,128)(2,1)}, u32[]{:S(2)}, u32[]{:S(2)}) collective-permute-start(bf16[1664,128]{1,0:T(8,128)(2,1)} %slice.24), channel_id=1, source_target_pairs={{0,1},{1,2},{2,3},{3,0},{4,5},{5,6},{6,7},{7,4},{8,9},{9,10},{10,1... | collective-permute-start | bytes 1277960 | tf_op jit(solution)/shard_map/ppermute | solution.py:352
  43.6 0.8 slice.25
  44.3 4.6 %collective-permute-start.8 = (bf16[1664,128]{1,0:T(8,128)(2,1)}, bf16[1664,128]{1,0:T(8,128)(2,1)}, u32[]{:S(2)}, u32[]{:S(2)}) collective-permute-start(bf16[1664,128]{1,0:T(8,128)(2,1)} %slice.25), channel_id=1, source_target_pairs={{0,3},{1,0},{2,1},{3,2},{4,7},{5,4},{6,5},{7,6},{8,11},{9,8},{10,9... | collective-permute-start | bytes 1277960 | tf_op jit(solution)/shard_map/ppermute | solution.py:352
  48.9 9.0 %all_to_all.72.wg_ref.refs_6_ = bf16[4,64,256]{2,1,0:T(8,128)(2,1)S(1)} all-to-all(bf16[4,64,256]{2,1,0:T(8,128)(2,1)S(1)} %broadcast_in_dim.51), channel_id=1, replica_groups=mesh['month_z'=16,'month_y'=4,'month_k'=2,'col'=4] {'col'}, dimensions={0} | all-to-all | bytes 262144 | tf_op jit(solution)/shard_map/all_to_all | solution.py:32
  58.0 1.2 shard_map.180
  59.1 9.9 %all_to_all.73.pieces_ref = f32[8,16,128]{2,1,0:T(8,128)S(1)} all-to-all(f32[8,16,128]{2,1,0:T(8,128)S(1)} %bitcast.127), channel_id=1, replica_groups=mesh['month_z'=16,'month_y'=4,'month_k'=2,'col'=4] {'month_y','month_k'}, dimensions={0} | all-to-all | bytes 131072 | tf_op jit(solution)/shard_map/all_to_all | solution.py:32
  69.0 0.7 shard_map.181
  69.7 14.7 %all-to-all-start.9 = ((f32[16,16,128]{2,1,0:T(8,128)}), f32[16,16,128]{2,1,0:T(8,128)S(1)}, u32[]{:S(2)}, u32[]{:S(2)}) async-start(f32[16,16,128]{2,1,0:T(8,128)} %shard_map.181), calls=%async_computation.9 | async-start | bytes 262144 | tf_op jit(solution)/shard_map/all_to_all | solution.py:32
  84.4 5.0 %shard_map.185 = (bf16[1216,256]{1,0:T(8,128)(2,1)}, bf16[256,1024]{1,0:T(8,128)(2,1)S(1)}, f32[128,1024]{1,0:T(8,128)S(1)}) custom-call(s32[2]{0:T(128)S(1)} %pad_add_fusion.pos_ref, s32[2,8,8]{2,1,0:T(8,128)S(1)} %bitcast.149, bf16[3840,128]{1,0:T(8,128)(2,1)S(1)} %get-tuple-element.87.refs_0_, bf16[3840,128]{1,0:T(8,128)(2,1)S(1)} %collective-permute-done.5.refs_1_, ...), custom_call_target="tpu_custom_call" | custom-call | tf_op jit(solution)/shard_map/pallas_call | solution.py:222
  89.4 0.8 copy-done.1
  90.2 0.8 copy-done.3
  91.0 3.0 %collective-permute-start.9 = (bf16[1216,256]{1,0:T(8,128)(2,1)}, bf16[1216,256]{1,0:T(8,128)(2,1)}, u32[]{:S(2)}, u32[]{:S(2)}) collective-permute-start(bf16[1216,256]{1,0:T(8,128)(2,1)} %get-tuple-element.92), channel_id=1, source_target_pairs={{4,0},{8,4},{12,8},{16,12},{20,16},{24,20},{28,24},{32,28},{36,32}... | collective-permute-start | bytes 1867784 | tf_op jit(solution)/shard_map/ppermute | solution.py:28
  93.9 2.4 %all-to-all-done.9.pieces_ref = f32[16,16,128]{2,1,0:T(8,128)S(1)} async-done(((f32[16,16,128]{2,1,0:T(8,128)}), f32[16,16,128]{2,1,0:T(8,128)S(1)}, u32[]{:S(2)}, u32[]{:S(2)}) %all-to-all-start.9) | async-done | bytes 131104 | tf_op jit(solution)/shard_map/all_to_all | solution.py:32
  96.3 0.7 copy-done
  97.1 9.5 %all-to-all-start.10 = ((f32[32,16,128]{2,1,0:T(8,128)}), f32[32,16,128]{2,1,0:T(8,128)S(1)}, u32[]{:S(2)}, u32[]{:S(2)}) async-start(f32[32,16,128]{2,1,0:T(8,128)} %copy-done), calls=%async_computation.10 | async-start | bytes 524288 | tf_op jit(solution)/shard_map/all_to_all | solution.py:32
  106.6 8.9 %all-to-all-done.10.pieces_ref = f32[32,16,128]{2,1,0:T(8,128)S(1)} async-done(((f32[32,16,128]{2,1,0:T(8,128)}), f32[32,16,128]{2,1,0:T(8,128)S(1)}, u32[]{:S(2)}, u32[]{:S(2)}) %all-to-all-start.10) | async-done | bytes 262176 | tf_op jit(solution)/shard_map/all_to_all | solution.py:32
  115.5 0.6 shard_map.183
  116.8 1.0 copy-done.2
  117.8 1.0 copy-done.4
  118.9 5.2 %shard_map.186 = (f32[1216,256]{1,0:T(8,128)S(1)}, f32[1,1024,256]{2,1,0:T(8,128)S(1)}, f32[1,256,128]{2,1,0:T(8,128)S(1)}) custom-call(s32[2]{0:T(128)S(1)} %pad_add_fusion.pos_ref, s32[2,8,8]{2,1,0:T(8,128)S(1)} %bitcast.150, bf16[3840,128]{1,0:T(8,128)(2,1)S(1)} %get-tuple-element.87.refs_0_, bf16[3840,128]{1,0:T(8,128)(2,1)S(1)} %collective-permute-done.5.refs_1_, ...), custom_call_target="tpu_custom_call" | custom-call | tf_op jit(solution)/shard_map/pallas_call | solution.py:259
  124.2 2.4 %conditional.1 = (f32[1,1024,256]{2,1,0:T(8,128)S(1)}, f32[1,1024,256]{2,1,0:T(8,128)S(1)}, f32[1,64,256]{2,1,0:T(8,128)S(1)}, f32[1,256,128]{2,1,0:T(8,128)S(1)}, f32[1,256,128]{2,1,0:T(8,128)S(1)}) conditional(s32[]{:T(128)} %bitcast.43, (s32[2]{0:T(128)S(1)}, s32[8,8]{1,0:T(8,128)S(1)}, f32[1216,256]{1,0:T(8,128)S(1)}, ...), branch_computations={%region_0.0_spmd, %region_1.0_spmd} | conditional | flops 3156738304 | bytes 132797224 | solution.py:468
  124.3 2.1 %branch_0_fun.1 = (f32[1,1024,256]{2,1,0:T(8,128)S(1)}, f32[1,64,256]{2,1,0:T(8,128)S(1)}, f32[1,256,128]{2,1,0:T(8,128)S(1)}) custom-call(s32[2]{0:T(128)S(1)} %get-tuple-element.40.pos_ref, s32[8,8]{1,0:T(8,128)S(1)} %get-tuple-element.41.dpat_ref, f32[1216,256]{1,0:T(8,128)S(1)} %get-tuple-element.42.here_ref, ...), custom_call_target="tpu_custom_call" | custom-call | tf_op jit(solution)/shard_map/cond/branch_0_fun/pallas_call | solution.py:289
  126.7 0.9 copy-done.50
  127.6 0.3 copy-done.51
  (43 shorter events, 0.2 us)
Async XLA Ops:
  0.6 57.3 %copy-start.14 = (bf16[1,256,128]{2,1,0:T(8,128)(2,1)S(1)}, bf16[1,256,128]{2,1,0:T(8,128)(2,1)}, u32[]{:S(2)}) copy-start(bf16[1,256,128]{2,1,0:T(8,128)(2,1)} %b_ref.3) | copy-start | bytes 196612
  0.6 57.3 %copy-start.25 = (s32[1,2,8,8]{3,2,1,0:T(8,128)S(1)}, s32[1,2,8,8]{3,2,1,0:T(8,128)}, u32[]{:S(2)}) copy-start(s32[1,2,8,8]{3,2,1,0:T(8,128)} %param.21) | copy-start | bytes 1540
  0.7 48.3 %copy-start.18 = (bf16[1,64,256]{2,1,0:T(8,128)(2,1)S(1)}, bf16[1,64,256]{2,1,0:T(8,128)(2,1)}, u32[]{:S(2)}) copy-start(bf16[1,64,256]{2,1,0:T(8,128)(2,1)} %w_ref.1) | copy-start | bytes 98308
  0.7 9.2 %collective-permute-start.4 = (bf16[1,256,128]{2,1,0:T(8,128)(2,1)}, bf16[1,256,128]{2,1,0:T(8,128)(2,1)S(1)}, u32[]{:S(2)}, u32[]{:S(2)}) collective-permute-start(bf16[1,256,128]{2,1,0:T(8,128)(2,1)} %x_ref.1), channel_id=1, source_target_pairs={{0,4},{4,8},{8,12},{12,16},{16,20},{20,24},{24,28},{28,32},{32,36}... | collective-permute-start | bytes 196616 | tf_op jit(solution)/shard_map/ppermute | solution.py:28
  5.4 52.6 %copy-start.7 = (bf16[1,1024,256]{2,1,0:T(8,128)(2,1)S(1)}, bf16[1,1024,256]{2,1,0:T(8,128)(2,1)}, u32[]{:S(2)}) copy-start(bf16[1,1024,256]{2,1,0:T(8,128)(2,1)} %refs_5_.3) | copy-start | bytes 1572868
  12.6 30.9 %collective-permute-start.6 = (bf16[4352,128]{1,0:T(8,128)(2,1)S(1)}, bf16[4352,128]{1,0:T(8,128)(2,1)S(1)}, u32[]{:S(2)}, u32[]{:S(2)}) collective-permute-start(bf16[4352,128]{1,0:T(8,128)(2,1)S(1)} %get-tuple-element.88), channel_id=1, source_target_pairs={{0,3},{1,0},{2,1},{3,2},{4,7},{5,4},{6,5},{7,6},{8,11},{9,8},{10,9... | collective-permute-start | bytes 3342344 | tf_op jit(solution)/shard_map/ppermute | solution.py:352
  14.5 26.3 %collective-permute-start.5 = (bf16[3840,128]{1,0:T(8,128)(2,1)S(1)}, bf16[3840,128]{1,0:T(8,128)(2,1)S(1)}, u32[]{:S(2)}, u32[]{:S(2)}) collective-permute-start(bf16[3840,128]{1,0:T(8,128)(2,1)S(1)} %get-tuple-element.87.refs_0_), channel_id=1, source_target_pairs={{0,1},{1,2},{2,3},{3,0},{4,5},{5,6},{6,7},{7,4},{8,9},{9,10},{10,1... | collective-permute-start | bytes 2949128 | tf_op jit(solution)/shard_map/ppermute | solution.py:352
  41.6 42.7 %collective-permute-start.7 = (bf16[1664,128]{1,0:T(8,128)(2,1)}, bf16[1664,128]{1,0:T(8,128)(2,1)}, u32[]{:S(2)}, u32[]{:S(2)}) collective-permute-start(bf16[1664,128]{1,0:T(8,128)(2,1)} %slice.24), channel_id=1, source_target_pairs={{0,1},{1,2},{2,3},{3,0},{4,5},{5,6},{6,7},{7,4},{8,9},{9,10},{10,1... | collective-permute-start | bytes 1277960 | tf_op jit(solution)/shard_map/ppermute | solution.py:352
  44.3 40.0 %collective-permute-start.8 = (bf16[1664,128]{1,0:T(8,128)(2,1)}, bf16[1664,128]{1,0:T(8,128)(2,1)}, u32[]{:S(2)}, u32[]{:S(2)}) collective-permute-start(bf16[1664,128]{1,0:T(8,128)(2,1)} %slice.25), channel_id=1, source_target_pairs={{0,3},{1,0},{2,1},{3,2},{4,7},{5,4},{6,5},{7,6},{8,11},{9,8},{10,9... | collective-permute-start | bytes 1277960 | tf_op jit(solution)/shard_map/ppermute | solution.py:352
  69.7 26.6 %all-to-all-start.9 = ((f32[16,16,128]{2,1,0:T(8,128)}), f32[16,16,128]{2,1,0:T(8,128)S(1)}, u32[]{:S(2)}, u32[]{:S(2)}) async-start(f32[16,16,128]{2,1,0:T(8,128)} %shard_map.181), calls=%async_computation.9 | async-start | bytes 262144 | tf_op jit(solution)/shard_map/all_to_all | solution.py:32
  84.3 31.2 %copy-start.5 = (f32[64,64]{1,0:T(8,128)S(1)}, f32[64,64]{1,0:T(8,128)}, u32[]{:S(2)}) copy-start(f32[64,64]{1,0:T(8,128)} %block_ref.1) | copy-start | bytes 49156
  84.3 31.1 %copy-start.6 = (f32[64,128]{1,0:T(8,128)S(1)}, f32[64,128]{1,0:T(8,128)}, u32[]{:S(2)}) copy-start(f32[64,128]{1,0:T(8,128)} %load_ref.1) | copy-start | bytes 98308
  89.4 0.8 copy-start.1
  90.2 0.8 copy-start.3
  91.0 33.2 %collective-permute-start.9 = (bf16[1216,256]{1,0:T(8,128)(2,1)}, bf16[1216,256]{1,0:T(8,128)(2,1)}, u32[]{:S(2)}, u32[]{:S(2)}) collective-permute-start(bf16[1216,256]{1,0:T(8,128)(2,1)} %get-tuple-element.92), channel_id=1, source_target_pairs={{4,0},{8,4},{12,8},{16,12},{20,16},{24,20},{28,24},{32,28},{36,32}... | collective-permute-start | bytes 1867784 | tf_op jit(solution)/shard_map/ppermute | solution.py:28
  96.3 0.7 copy-start
  97.1 18.4 %all-to-all-start.10 = ((f32[32,16,128]{2,1,0:T(8,128)}), f32[32,16,128]{2,1,0:T(8,128)S(1)}, u32[]{:S(2)}, u32[]{:S(2)}) async-start(f32[32,16,128]{2,1,0:T(8,128)} %copy-done), calls=%async_computation.10 | async-start | bytes 524288 | tf_op jit(solution)/shard_map/all_to_all | solution.py:32
  116.8 1.0 copy-start.2
  117.8 1.0 copy-start.4
  118.9 5.3 %copy-start.15 = (bf16[1,256,128]{2,1,0:T(8,128)(2,1)S(1)}, bf16[1,256,128]{2,1,0:T(8,128)(2,1)}, u32[]{:S(2)}) copy-start(bf16[1,256,128]{2,1,0:T(8,128)(2,1)} %b_ref.3) | copy-start | bytes 196612
  118.9 5.3 %copy-start.19 = (bf16[1,64,256]{2,1,0:T(8,128)(2,1)S(1)}, bf16[1,64,256]{2,1,0:T(8,128)(2,1)}, u32[]{:S(2)}) copy-start(bf16[1,64,256]{2,1,0:T(8,128)(2,1)} %w_ref.1) | copy-start | bytes 98308
  118.9 5.3 %copy-start.20 = (bf16[1,256,128]{2,1,0:T(8,128)(2,1)S(1)}, bf16[1,256,128]{2,1,0:T(8,128)(2,1)}, u32[]{:S(2)}) copy-start(bf16[1,256,128]{2,1,0:T(8,128)(2,1)} %x_ref.1) | copy-start | bytes 196612
  118.9 5.3 %copy-start.27 = (bf16[1,256,128]{2,1,0:T(8,128)(2,1)S(1)}, bf16[1,256,128]{2,1,0:T(8,128)(2,1)}, u32[]{:S(2)}) copy-start(bf16[1,256,128]{2,1,0:T(8,128)(2,1)} %param.23) | copy-start | bytes 196612
  118.9 5.3 %copy-start.38 = (bf16[1,64,256]{2,1,0:T(8,128)(2,1)S(1)}, bf16[1,64,256]{2,1,0:T(8,128)(2,1)}, u32[]{:S(2)}) copy-start(bf16[1,64,256]{2,1,0:T(8,128)(2,1)} %param.19) | copy-start | bytes 98308
  118.9 5.3 %copy-start.46 = (s32[1,8,8]{2,1,0:T(8,128)S(1)}, s32[1,8,8]{2,1,0:T(8,128)}, u32[]{:S(2)}) copy-start(s32[1,8,8]{2,1,0:T(8,128)} %param.20) | copy-start | bytes 772
  126.6 1.0 copy-start.50
  126.6 1.3 %copy-start.51 = (f32[1,1024,256]{2,1,0:T(8,128)}, f32[1,1024,256]{2,1,0:T(8,128)S(1)}, u32[]{:S(2)}) copy-start(f32[1,1024,256]{2,1,0:T(8,128)S(1)} %get-tuple-element.127) | copy-start | bytes 3145732
  126.6 1.3 %copy-start.52 = (f32[1,256,128]{2,1,0:T(8,128)}, f32[1,256,128]{2,1,0:T(8,128)S(1)}, u32[]{:S(2)}) copy-start(f32[1,256,128]{2,1,0:T(8,128)S(1)} %get-tuple-element.134) | copy-start | bytes 393220
  126.7 1.4 %copy-start.53 = (f32[1,256,128]{2,1,0:T(8,128)}, f32[1,256,128]{2,1,0:T(8,128)S(1)}, u32[]{:S(2)}) copy-start(f32[1,256,128]{2,1,0:T(8,128)S(1)} %get-tuple-element.130) | copy-start | bytes 393220
  126.7 1.4 %copy-start.54 = (f32[1,64,256]{2,1,0:T(8,128)}, f32[1,64,256]{2,1,0:T(8,128)S(1)}, u32[]{:S(2)}) copy-start(f32[1,64,256]{2,1,0:T(8,128)S(1)} %get-tuple-element.129) | copy-start | bytes 196612
